TPU v7x, 512 devices: a whole 4x8x8 slice. The times are simulated.
512 devices in a mesh: dp: 32 (over x, y), region: 16 (over z, core).
Axes of the slice: x: 4, y: 8, z: 8, core: 2. Of those that a mesh axis runs over, the one named last changes fastest.
Arguments:
- inputs: bfloat16 [32, 2, 4096, 256], P('dp', None, 'region'), may hold values from -6 to 6
- cotangent: bfloat16 [32, 2, 4096, 256], P('dp', None, 'region'), may hold values from -6 to 6
- w_filter: bfloat16 [2, 256, 256], replicated, may hold values from -0.25 to 0.25
- w_gate: bfloat16 [2, 256, 256], replicated, may hold values from -0.25 to 0.25
- w_mix: bfloat16 [2, 256, 256], replicated, may hold values from -0.25 to 0.25
- neighbours: int32 [32, 6], replicated, may hold values from 0 to 31, as said below
- adjacency: bfloat16 [32, 6, 128, 128], P('region'), may hold values from -0.21875 to 0.21875
Outputs:
- grad_inputs: bfloat16 [32, 2, 4096, 256], P('dp', None, 'region')
- grad_filter: float32 [2, 256, 256], replicated
- grad_gate: float32 [2, 256, 256], replicated
- grad_mix: float32 [2, 256, 256], replicated
Inputs may be any that keep to these rules, and one draw needn't show every extreme that they name: `neighbours`: for every region r (tiles r * 2 to (r + 1) * 2 - 1), exactly 11 of the 12 entries of its tiles' lists name tiles of other regions, each of a different region, so at most 1 name tiles of any one other region; all other entries name tiles of region r.
All inputs are finite; a program needn't handle non-finite values.
Results may differ from a plain program's by a relative error of at most 0.0053.
Values may be sent and summed in bfloat16 or wider, within the bound.
A program may use at most 64 MiB of HBM per device.

v0:
```python
import math

import jax
import jax.numpy as jnp
from jax import lax
from jax.sharding import PartitionSpec as P

CAP = 1


def per_device(inputs, cotangent, w_filter, w_gate, w_mix, neighbours, adjacency):
    regions = lax.axis_size("region")
    region_id = lax.axis_index("region")
    windows, steps, site_count, chans = inputs.shape
    tiles_dev = site_count // 128
    per_tile = neighbours.shape[1]
    entries = tiles_dev * per_tile
    capacity = CAP
    table = neighbours.reshape(regions, entries)
    owners = table // tiles_dev
    local_tile = table % tiles_dev
    sources = jnp.arange(regions, dtype=jnp.int32)
    positions = jnp.arange(entries)
    earlier = positions[:, None] > positions[None, :]
    ranks = jnp.sum(
        ((owners[:, :, None] == owners[:, None, :]) & earlier[None]).astype(jnp.int32), axis=2
    )
    slot_ids = jnp.arange(capacity)
    remote_entry = owners != sources[:, None]
    hits = (
        (owners[:, None, :] == region_id)
        & (ranks[:, None, :] == slot_ids[None, :, None])
        & remote_entry[:, None, :]
    )
    send_tile = jnp.sum(jnp.where(hits, local_tile[:, None, :], 0), axis=2).reshape(-1)
    send_used = jnp.any(hits, axis=2).reshape(-1)
    own_owner = lax.dynamic_index_in_dim(owners, region_id, 0, keepdims=False)
    own_rank = lax.dynamic_index_in_dim(ranks, region_id, 0, keepdims=False)
    own_tiles = lax.dynamic_index_in_dim(table, region_id, 0, keepdims=False)
    own_local_tile = lax.dynamic_index_in_dim(local_tile, region_id, 0, keepdims=False)
    at_home = own_owner == region_id
    drop_index = jnp.where(at_home, regions * capacity, own_owner * capacity + own_rank)
    w_cat = jnp.concatenate(
        [
            jnp.concatenate([w_filter[0], w_gate[0]], axis=1),
            jnp.concatenate([w_filter[1], w_gate[1]], axis=1),
        ],
        axis=0,
    )
    w_mixed = w_mix.reshape(2 * chans, chans)
    previous = jnp.concatenate([jnp.zeros_like(inputs[:, :1]), inputs[:, :-1]], axis=1)
    joint = jnp.concatenate([inputs, previous], axis=3)
    act = jnp.einsum("btsi,io->btso", joint, w_cat, preferred_element_type=jnp.float32)
    filt = jnp.tanh(act[..., :chans])
    gate = jax.nn.sigmoid(act[..., chans:])
    hidden = (filt * gate).astype(jnp.bfloat16)
    tiled = hidden.reshape(windows, steps, tiles_dev, 128, chans)
    piece = lax.all_gather(tiled, "region", axis=2, tiled=True)
    count = piece.shape[2]
    select = (own_tiles[:, None] == jnp.arange(count)[None, :]).astype(jnp.bfloat16)
    chosen = jnp.einsum("en,btnqc->bteqc", select, piece, preferred_element_type=jnp.float32)
    chosen = chosen.astype(jnp.bfloat16).reshape(windows, steps, tiles_dev, per_tile, 128, chans)
    graph_sum = jnp.einsum(
        "jkpq,btjkqc->btjpc", adjacency, chosen, preferred_element_type=jnp.float32
    )
    graph = graph_sum.astype(jnp.bfloat16).reshape(windows, steps, site_count, chans)
    both = jnp.concatenate([hidden, graph], axis=3)
    mix_sum = jnp.einsum("btsi,btsc->ic", both, cotangent, preferred_element_type=jnp.float32)
    back = jnp.einsum("btsc,ic->btsi", cotangent, w_mixed, preferred_element_type=jnp.float32)
    direct = back[..., :chans]
    graph_cot = (
        back[..., chans:].astype(jnp.bfloat16).reshape(windows, steps, tiles_dev, 128, chans)
    )
    term = jnp.einsum(
        "jkpq,btjpc->btjkqc", adjacency, graph_cot, preferred_element_type=jnp.float32
    )
    term = term.astype(jnp.bfloat16).reshape(windows, steps, entries, 128, chans)
    outgoing_back = jnp.zeros((windows, steps, regions * capacity, 128, chans), jnp.bfloat16)
    outgoing_back = outgoing_back.at[:, :, drop_index].set(term, mode="drop")
    outgoing_back = outgoing_back.reshape(windows, steps, regions, capacity, 128, chans)
    returned = lax.all_to_all(outgoing_back, "region", split_axis=2, concat_axis=2, tiled=True)
    returned = returned.reshape(windows, steps, regions * capacity, 128, chans)
    owner_hot = (
        (send_tile[None, :] == jnp.arange(tiles_dev)[:, None]) & send_used[None, :]
    ).astype(jnp.bfloat16)
    graph_grad = jnp.einsum(
        "ln,btnqc->btlqc", owner_hot, returned, preferred_element_type=jnp.float32
    )
    home_hot = (
        (own_local_tile[None, :] == jnp.arange(tiles_dev)[:, None]) & at_home[None, :]
    ).astype(jnp.bfloat16)
    home_grad = jnp.einsum("le,bteqc->btlqc", home_hot, term, preferred_element_type=jnp.float32)
    grad_hidden = direct + (graph_grad + home_grad).reshape(windows, steps, site_count, chans)
    act_cot = jnp.concatenate(
        [grad_hidden * gate * (1.0 - filt * filt), grad_hidden * filt * gate * (1.0 - gate)], axis=3
    ).astype(jnp.bfloat16)
    conv_sum = jnp.einsum("btsi,btso->io", joint, act_cot, preferred_element_type=jnp.float32)
    back_in = jnp.einsum("btso,io->btsi", act_cot, w_cat, preferred_element_type=jnp.float32)
    later = jnp.concatenate(
        [back_in[:, 1:, :, chans:], jnp.zeros((windows, 1, site_count, chans), jnp.float32)], axis=1
    )
    grad_inputs = (cotangent.astype(jnp.float32) + back_in[..., :chans] + later).astype(
        jnp.bfloat16
    )
    conv_total, mix_total = lax.psum((conv_sum, mix_sum), ("dp", "region"))
    total_rows = windows * lax.axis_size("dp") * steps * site_count * regions
    factor = 1.0 / math.sqrt(total_rows)
    grad_filter = (conv_total[:, :chans] * factor).reshape(2, chans, chans)
    grad_gate = (conv_total[:, chans:] * factor).reshape(2, chans, chans)
    grad_mix = (mix_total * factor).reshape(2, chans, chans)
    return (grad_inputs, grad_filter, grad_gate, grad_mix)


def solution(mesh):
    return jax.shard_map(
        per_device,
        mesh=mesh,
        in_specs=(
            P("dp", None, "region", None),
            P("dp", None, "region", None),
            P(),
            P(),
            P(),
            P(),
            P("region", None, None, None),
        ),
        out_specs=(P("dp", None, "region", None), P(), P(), P()),
        check_vma=False,
    )
```

profile of v0, /device:TPU:1, one launch (start us, length us, event | category | flops | bytes accessed | tf_op | source)
XLA Modules:
  0.0 428.7 jit_solution(3742528526093285278)
XLA Ops:
  7.2 0.0 copy-start
  7.2 0.8 copy.73
  8.0 0.1 reshape.354
  8.1 0.6 copy-done.15
  8.7 0.1 copy.74
  8.8 0.6 negate_select_fusion.4
  9.4 0.1 copy.78
  9.5 0.8 fusion.81
  10.2 0.4 convert_reduce_fusion
  10.6 0.2 select_reduce_fusion
  10.8 0.6 fusion.70
  11.4 1.3 convolution_bitcast_fusion
  12.8 0.9 copy-done.1
  13.7 0.6 fusion.12
  14.3 0.7 copy.80
  15.0 0.1 copy.81
  15.2 1.6 broadcast.246
  16.8 5.3 %scatter_fusion = bf16[2,16,128,256]{3,2,1,0:T(8,128)(2,1)} fusion(bf16[2,16,128,256]{3,2,1,0:T(8,128)(2,1)} %broadcast.246, s32[12]{0:T(128)} %fusion.70, bf16[12,2,128,256]{3,2,1,0:T(8,128)(2,1)S(1)} %copy.81), kind=kCustom, calls=%fused_computation | custom fusion | bytes 4718640 | tf_op jit(solution)/shard_map/scatter | solution.py:79
  22.1 3.1 copy.82
  25.3 11.9 %all-to-all-start = ((bf16[1,2,16,1,128,256]{5,4,1,3,0,2:T(8,128)(2,1)}), bf16[1,2,16,1,128,256]{5,4,1,3,0,2:T(8,128)(2,1)}, u32[]{:S(2)}, u32[]{:S(2)}) async-start(bf16[1,2,16,1,128,256]{5,4,1,3,0,2:T(8,128)(2,1)} %copy.82), calls=%async_computation | async-start | bytes 4194304 | tf_op jit(solution)/shard_map/all_to_all | solution.py:81
  37.2 0.0 all-gather.2.cloned.1.call-start
  37.3 0.1 reshape.359
  37.3 0.1 copy.85
  37.5 0.2 fusion.51
  37.8 0.6 copy-done.7
  38.4 1.4 convolution_bitcast_fusion.3
  39.8 46.4 %all-to-all-done = bf16[1,2,16,1,128,256]{5,4,1,3,0,2:T(8,128)(2,1)} async-done(((bf16[1,2,16,1,128,256]{5,4,1,3,0,2:T(8,128)(2,1)}), bf16[1,2,16,1,128,256]{5,4,1,3,0,2:T(8,128)(2,1)}, u32[]{:S(2)}, u32[]{:S(2)}) %all-to-all-start) | async-done | bytes 2097184 | tf_op jit(solution)/shard_map/all_to_all | solution.py:81
  86.3 2.9 fusion.3
  89.1 1.1 fusion.19
  90.3 0.1 copy-done.2
  90.4 0.3 fusion.42
  90.7 0.7 copy.92
  91.4 0.0 all-gather.2.cloned.1.call-update
  91.4 0.0 all-reduce.5.cloned.1.call-start
  91.5 0.7 fusion.69
  92.2 1.4 convolution_bitcast_fusion.1
  93.6 42.7 %all-gather.2.cloned.1.call-done = bf16[1,2,32,128,256]{4,3,1,0,2:T(8,128)(2,1)} async-done(((bf16[1,2,2,128,256]{4,3,1,0,2:T(8,128)(2,1)}), bf16[1,2,32,128,256]{4,3,1,0,2:T(8,128)(2,1)}) %all-gather.2.cloned.1.call-update) | async-done | bytes 4194320 | tf_op jit(solution)/shard_map/all_gather | solution.py:58
  136.3 4.7 %convert_bitcast_fusion = bf16[1,2,12,128,256]{4,2,3,1,0:T(8,128)(2,1)S(1)} fusion(bf16[1,2,32,128,256]{4,3,1,0,2:T(8,128)(2,1)} %all-gather.2.cloned.1.call-done, s32[12]{0:T(128)S(1)} %fusion.69), kind=kOutput, calls=%fused_computation.9 | convolution fusion | flops 51118464 | bytes 5767216 | tf_op jit(solution)/shard_map/en,btnqc->bteqc/dot_general | solution.py:61
  141.0 0.6 copy.94
  141.6 0.4 fusion.25
  142.0 0.5 copy-done.3
  142.5 1.1 convolution_bitcast_fusion.4
  143.6 0.0 all-reduce.5.cloned.1.call-update
  143.7 0.5 convolution_bitcast_fusion.2
  144.2 0.8 fusion.32
  145.0 273.7 %all-reduce.5.cloned.1.call-done = (f32[512,512]{1,0:T(8,128)}, f32[512,256]{1,0:T(8,128)}) async-done(((f32[512,512]{1,0:T(8,128)}, f32[512,256]{1,0:T(8,128)}), (f32[512,512]{1,0:T(8,128)}, f32[512,256]{1,0:T(8,128)})) %all-reduce.5.cloned.1.call-update) | async-done | bytes 1572880 | tf_op jit(solution)/shard_map/psum | solution.py:105
  418.7 2.3 slice_multiply_fusion
  421.0 0.8 broadcast_multiply_fusion
  (40 shorter events, 0.3 us)
Async XLA Ops:
  7.2 6.5 %copy-start = (bf16[2,6,128,128]{3,2,1,0:T(8,128)(2,1)S(1)}, bf16[2,6,128,128]{3,2,1,0:T(8,128)(2,1)}, u32[]{:S(2)}) copy-start(bf16[2,6,128,128]{3,2,1,0:T(8,128)(2,1)} %param.13) | copy-start | bytes 1179652
  8.1 0.6 copy-start.15
  8.8 4.9 %copy-start.9 = (s32[16,12]{0,1:T(8,128)}, s32[16,12]{0,1:T(8,128)S(1)}, u32[]{:S(2)}) copy-start(s32[16,12]{0,1:T(8,128)S(1)} %copy.74) | copy-start | bytes 2308
  10.6 3.1 copy-start.11
  12.7 1.0 copy-start.1
  25.2 12.2 %copy-start.13 = (bf16[1,2,256,256]{3,2,1,0:T(8,128)(2,1)S(1)}, bf16[1,2,256,256]{3,2,1,0:T(8,128)(2,1)}, u32[]{:S(2)}) copy-start(bf16[1,2,256,256]{3,2,1,0:T(8,128)(2,1)} %param.7) | copy-start | bytes 786436
  25.2 12.2 %copy-start.12 = (s32[16,12]{0,1:T(8,128)S(1)}, s32[16,12]{0,1:T(8,128)}, u32[]{:S(2)}) copy-start(s32[16,12]{0,1:T(8,128)} %copy-done.11) | copy-start | bytes 2308
  25.2 12.3 %copy-start.10 = (s32[16,12]{0,1:T(8,128)S(1)}, s32[16,12]{0,1:T(8,128)}, u32[]{:S(2)}) copy-start(s32[16,12]{0,1:T(8,128)} %copy-done.9) | copy-start | bytes 2308
  25.2 12.3 %copy-start.16 = (s32[16,12]{0,1:T(8,128)S(1)}, s32[16,12]{0,1:T(8,128)}, u32[]{:S(2)}) copy-start(s32[16,12]{0,1:T(8,128)} %get-tuple-element.19) | copy-start | bytes 2308
  25.2 12.5 %copy-start.5 = (bf16[2,256,256]{2,1,0:T(8,128)(2,1)S(1)}, bf16[2,256,256]{2,1,0:T(8,128)(2,1)}, u32[]{:S(2)}) copy-start(bf16[2,256,256]{2,1,0:T(8,128)(2,1)} %param.10) | copy-start | bytes 786436
  25.2 12.5 %copy-start.6 = (bf16[2,256,256]{2,1,0:T(8,128)(2,1)S(1)}, bf16[2,256,256]{2,1,0:T(8,128)(2,1)}, u32[]{:S(2)}) copy-start(bf16[2,256,256]{2,1,0:T(8,128)(2,1)} %param.9) | copy-start | bytes 786436
  25.3 61.0 %all-to-all-start = ((bf16[1,2,16,1,128,256]{5,4,1,3,0,2:T(8,128)(2,1)}), bf16[1,2,16,1,128,256]{5,4,1,3,0,2:T(8,128)(2,1)}, u32[]{:S(2)}, u32[]{:S(2)}) async-start(bf16[1,2,16,1,128,256]{5,4,1,3,0,2:T(8,128)(2,1)} %copy.82), calls=%async_computation | async-start | bytes 4194304 | tf_op jit(solution)/shard_map/all_to_all | solution.py:81
  37.2 99.1 %all-gather.2.cloned.1.call-start = ((), (), s32[]{:S(2)}) async-start(), calls=%async_computation.1 | async-start | bytes 4456448 | tf_op jit(solution)/shard_map/all_gather | solution.py:58
  37.8 0.7 copy-start.7
  39.8 49.3 %copy-start.17 = (pred[12]{0:T(512)(128)(4,1)S(1)}, pred[12]{0:T(512)(128)(4,1)}, u32[]{:S(2)}) copy-start(pred[12]{0:T(512)(128)(4,1)} %get-tuple-element.6) | copy-start | bytes 40
  89.1 1.2 copy-start.2
  90.4 1.8 copy-start.14
  91.4 327.3 %all-reduce.5.cloned.1.call-start = ((), (), s32[]{:S(2)}) async-start(), calls=%async_computation.2 | async-start | bytes 3145728 | tf_op jit(solution)/shard_map/psum | solution.py:105
  141.5 1.0 copy-start.3
  141.9 1.7 copy-start.8
  418.7 2.3 copy-start.4
Sparse Core Ops, SparseCore 0:
  91.5 44.7 all-gather.1
  143.8 274.8 all-reduce.4
where the time goes:
time: 430 us; the launch traced here: 429 us
  waiting for transfers between devices  363 us (84%)
  local copies, waits for them, and re-layouts  17 us (4%)
  matrix products  15.4 us (4%)
  between operations  14.3 us (3%)
  starting transfers between devices  12 us (3%)
  other arithmetic  6.99 us (2%)
    psum x1, waiting for transfers between devices, per_device(): conv_total, mix_total = lax.psum((conv_sum, mix_sum), ('dp', 'region'))  274 us
    all_to_all x1, waiting for transfers between devices, per_device(): lax.all_to_all(outgoing_back, 'region', split_axis=2, concat_axis=2, tile...  46.4 us
    all_gather x1, waiting for transfers between devices, per_device(): piece = lax.all_gather(tiled, 'region', axis=2, tiled=True)  42.7 us
    all_to_all x1, starting transfers between devices, per_device(): lax.all_to_all(outgoing_back, 'region', split_axis=2, concat_axis=2, tile...  11.9 us
  transfers between devices with their start and end apart: 3, of which 3 were waited for; matrix products, arithmetic and copies ran while one was open for 1% of the time, Pallas kernels for 0%

commit v1 on v0

v1 whole, which is shorter than its diff:
```python
import functools
import math

import jax
import jax.numpy as jnp
from jax import lax
from jax.experimental import pallas as pl
from jax.experimental.pallas import tpu as pltpu
from jax.sharding import PartitionSpec as P

MESH = pl.DeviceIdType.MESH
X = 4
TILE = 128
F32 = jnp.float32
BF16 = jnp.bfloat16


def dot(a, b, contract):
    return lax.dot_general(a, b, ((contract[:1], contract[1:]), ((), ())), preferred_element_type=F32)


class Reduction:
    def __init__(self, place, part, base, factor, scratch, sems, sends):
        self.place, self.part, self.base, self.factor, self.sends = place, part, base, factor, sends
        self.core, self.ysend, self.yrecv, self.xs, self.xrecv, self.zrecv, self.xg, self.yg, self.cg = scratch
        self.send, self.recv = sems
        self.count = self.core.shape[0]

    def copy(self, src, dst, sem, device):
        item = pltpu.make_async_remote_copy(
            src_ref=src, dst_ref=dst, send_sem=self.send.at[sem], recv_sem=self.recv.at[sem],
            device_id=device, device_id_type=MESH,
        )
        item.start()
        self.sends.append(item)
        return item

    def wait(self, items):
        for item in items:
            item.wait_recv()

    def start_core(self):
        p = self.place
        half = TILE
        other = pl.ds(pl.multiple_of((1 - p.c) * half, half), half)
        self.items = [self.copy(self.part.at[pl.ds(self.base, self.count), other], self.core, 0, p.sibling)]

    def start_y(self):
        p = self.place
        self.wait(self.items)
        rows = TILE // p.Y
        mine = pl.ds(pl.multiple_of(p.c * TILE, TILE), TILE)
        for i in range(self.count):
            total = self.core[i] + self.part[self.base + i, mine]
            self.core[i] = total
            self.ysend[:, i] = total.astype(BF16).reshape(p.Y, rows, total.shape[-1])
        self.items = [
            self.copy(self.ysend.at[lax.rem(p.y + i, p.Y)], self.yrecv.at[i - 1], i, p.along_y(i))
            for i in range(1, p.Y)
        ]

    def start_x(self):
        p = self.place
        self.wait(self.items)
        rows = TILE // p.Y
        half = rows // 2
        for i in range(self.count):
            total = self.core[i, pl.ds(pl.multiple_of(p.y * rows, rows), rows)]
            for j in range(p.Y - 1):
                total = total + self.yrecv[j, i].astype(F32)
            for q in range(X):
                top, left = (q // 2) * half, (q % 2) * 128
                self.xs[q, i] = total[top:top + half, left:left + 128]
        self.items = [
            self.copy(self.xs.at[lax.rem(p.x + i, X)], self.xrecv.at[i - 1], p.Y + i, p.along_x(i))
            for i in range(1, X)
        ]

    def start_z(self):
        p = self.place
        self.wait(self.items)
        total = self.xs[p.x]
        for j in range(X - 1):
            total = total + self.xrecv[j]
        self.zrecv[p.z] = total
        self.items = [
            self.copy(self.zrecv.at[p.z], self.zrecv.at[p.z], p.Y + X + i, p.along_z(i))
            for i in range(1, p.Z)
        ]

    def start_gather_x(self):
        p = self.place
        self.wait(self.items)
        total = self.zrecv[0]
        for j in range(1, p.Z):
            total = total + self.zrecv[j]
        self.xg[p.x] = total * self.factor
        self.items = [
            self.copy(self.xg.at[p.x], self.xg.at[p.x], p.Y + X + p.Z + i, p.along_x(i))
            for i in range(1, X)
        ]

    def start_gather_y(self):
        p = self.place
        self.wait(self.items)
        for i in range(self.count):
            rows = [jnp.concatenate([self.xg[2 * r, i], self.xg[2 * r + 1, i]], axis=1) for r in range(2)]
            self.yg[p.y, i] = jnp.concatenate(rows, axis=0).astype(BF16)
        self.items = [
            self.copy(self.yg.at[p.y], self.yg.at[p.y], p.Y + 2 * X + p.Z + i, p.along_y(i))
            for i in range(1, p.Y)
        ]

    def start_gather_core(self):
        p = self.place
        self.wait(self.items)
        self.items = [self.copy(self.yg, self.cg, 2 * p.Y + 2 * X + p.Z, p.sibling)]

    def finish(self, outs):
        p = self.place
        for source, core in ((self.yg, p.c), (self.cg, 1 - p.c)):
            if source is self.cg:
                self.wait(self.items)
            rows = pl.ds(pl.multiple_of(core * TILE, TILE), TILE)
            for i, (ref, tap) in enumerate(outs):
                block = source[:, i].reshape(TILE, ref.shape[-1])
                ref[tap, rows] = block.astype(F32)


class Place:
    def __init__(self, Y, Z):
        self.Y, self.Z = Y, Z
        self.dp = lax.axis_index("dp")
        self.region = lax.axis_index("region")
        self.x, self.y = lax.div(self.dp, Y), lax.rem(self.dp, Y)
        self.z, self.c = lax.div(self.region, 2), lax.rem(self.region, 2)
        self.sibling = (self.dp, self.z * 2 + 1 - self.c)

    def along_x(self, i):
        return (lax.rem(self.x + i, X) * self.Y + self.y, self.region)

    def along_y(self, i):
        return (self.x * self.Y + lax.rem(self.y + i, self.Y), self.region)

    def along_z(self, i):
        return (self.dp, lax.rem(self.z + i, self.Z) * 2 + self.c)


def kernel(Y, Z, factor, nbr, x_ref, cot_ref, wf, wg, wm, adj,
           gi_ref, gf_ref, gg_ref, gm_ref,
           gall, hall, asend, arecv, afull, bmat, fmat, acc, hacc, f1, f2, actcot, part, table, *rest):
    big, small = rest[:9], rest[9:18]
    ring_send, ring_recv, sib_send, sib_recv, adj_send, adj_recv, big_send, big_recv, small_send, small_recv = rest[18:]
    p = Place(Y, Z)
    R = 2 * Z
    per_tile = nbr.shape[1]
    entries = 2 * per_tile
    rows = TILE // Y
    sends = []

    barrier = pltpu.get_barrier_semaphore()
    partners = [(p.dp, lax.rem(p.region + i, R)) for i in range(1, R)]
    partners += [p.along_y(i) for i in range(1, Y)] + [p.along_x(i) for i in range(1, X)]
    for device in partners:
        pl.semaphore_signal(barrier, inc=1, device_id=device, device_id_type=MESH)

    def remote(src, dst, send, recv, device):
        item = pltpu.make_async_remote_copy(
            src_ref=src, dst_ref=dst, send_sem=send, recv_sem=recv, device_id=device, device_id_type=MESH)
        item.start()
        sends.append(item)

    def arrived(ref, send, recv):
        pltpu.make_async_remote_copy(
            src_ref=ref, dst_ref=ref, send_sem=send, recv_sem=recv, device_id=p.sibling, device_id_type=MESH
        ).wait_recv()

    def origin(direction, step):
        return lax.rem(p.z + (Z - step if direction == 0 else step), Z)

    def ring(stream, buf, step):
        for tile in range(2):
            for direction in range(2):
                slot = origin(direction, step) * 2 + p.c
                block = buf.at[direction, slot, tile]
                if step > 0:
                    arrived(block, ring_send.at[stream, direction, step - 1, tile],
                            ring_recv.at[stream, direction, step - 1, tile])
                if step < Z - 1:
                    remote(block, block, ring_send.at[stream, direction, step, tile],
                           ring_recv.at[stream, direction, step, tile], p.along_z(1 if direction == 0 else Z - 1))
                remote(block, block, sib_send.at[stream, direction, step, tile],
                       sib_recv.at[stream, direction, step, tile], p.sibling)

    def from_sibling(stream, buf, step):
        for tile in range(2):
            for direction in range(2):
                slot = origin(direction, step) * 2 + 1 - p.c
                arrived(buf.at[direction, slot, tile], sib_send.at[stream, direction, step, tile],
                        sib_recv.at[stream, direction, step, tile])

    def pair(buf, t, chip, choice):
        halves = []
        for core in range(2):
            region = chip * 2 + core
            first = table[choice, region] == 0
            halves.append(jnp.where(first, buf[t, region, 0], buf[t, region, 1]))
        return jnp.concatenate(halves, axis=0)

    for t in range(2):
        gall[t, p.region] = dot(cot_ref[t], wm[1], (1, 1)).astype(BF16).reshape(2, TILE, -1)
    pl.semaphore_wait(barrier, len(partners))
    ring(0, gall, 0)

    def scan(region, carry):
        entry = valid = own = named = other = mine = jnp.int32(0)
        for e in range(entries):
            a = nbr[p.region * 2 + e // per_tile, e % per_tile]
            hit = lax.div(a, 2) == region
            entry = jnp.where(hit, e, entry)
            valid = jnp.where(hit, 1, valid)
            own = jnp.where(hit, e // per_tile, own)
            named = jnp.where(hit, lax.rem(a, 2), named)
            b = nbr[region * 2 + e // per_tile, e % per_tile]
            back = lax.div(b, 2) == p.region
            other = jnp.where(back, e // per_tile, other)
            mine = jnp.where(back, lax.rem(b, 2), mine)
        for row, value in enumerate((entry, valid, own, named, other, mine)):
            table[row, region] = value
        return carry
    lax.fori_loop(0, R, scan, 0)

    def fill(region, carry):
        block = adj[table[0, region], pl.ds(pl.multiple_of(p.y * rows, rows), rows)]
        asend[region] = jnp.where(table[1, region] == 1, block, jnp.zeros_like(block))
        return carry
    lax.fori_loop(0, R, fill, 0)
    arecv[p.region] = asend[p.region]
    for i in range(1, R):
        target = lax.rem(p.region + i, R)
        remote(asend.at[target], arecv.at[p.region], adj_send.at[i], adj_recv.at[i], (p.dp, target))

    for t in range(2):
        pre_f = dot(x_ref[t], wf[0], (1, 0))
        pre_g = dot(x_ref[t], wg[0], (1, 0))
        if t == 1:
            pre_f = pre_f + dot(x_ref[0], wf[1], (1, 0))
            pre_g = pre_g + dot(x_ref[0], wg[1], (1, 0))
        filt = jnp.tanh(pre_f)
        gate = jax.nn.sigmoid(pre_g)
        both = filt * gate
        hall[t, p.region] = both.astype(BF16).reshape(2, TILE, -1)
        f1[t] = gate * (1.0 - filt * filt)
        f2[t] = both * (1.0 - gate)
    ring(0, gall, 1)

    for i in range(1, R):
        source = lax.rem(p.region + R - i, R)
        arrived(arecv.at[source], adj_send.at[i], adj_recv.at[i])
    afull[p.y] = arecv[...]
    for i in range(1, Y):
        remote(arecv, afull.at[p.y], adj_send.at[R + i], adj_recv.at[R + i], p.along_y(i))
    for t in range(2):
        acc[t] = dot(cot_ref[t], wm[0], (1, 1))
        own = hall[t, p.region].reshape(2 * TILE, -1)
        here = dot(own, cot_ref[t], (0, 0))
        part[4] = here if t == 0 else part[4] + here
    ring(0, gall, 2)

    def build_forward(chip, carry):
        for core in range(2):
            region = chip * 2 + core
            block = adj[table[0, region]]
            zero = jnp.zeros_like(block)
            own = jnp.where(table[1, region] == 1, table[2, region], 2)
            for j in range(2):
                fmat[chip, j * TILE:(j + 1) * TILE, core * TILE:(core + 1) * TILE] = jnp.where(own == j, block, zero)
        return carry
    lax.fori_loop(0, Z, build_forward, 0)
    for i in range(1, Y):
        source = lax.rem(p.y + Y - i, Y)
        arrived(afull.at[source], adj_send.at[R + i], adj_recv.at[R + i])

    def build_backward(chip, carry):
        for core in range(2):
            region = chip * 2 + core
            block = afull[:, region].reshape(TILE, TILE)
            zero = jnp.zeros_like(block)
            for j in range(2):
                bmat[chip, core * TILE:(core + 1) * TILE, j * TILE:(j + 1) * TILE] = jnp.where(
                    table[5, region] == j, block, zero)
        return carry
    lax.fori_loop(0, Z, build_backward, 0)

    def backward(step):
        from_sibling(0, gall, step)
        for t in range(2):
            chip = origin(t, step)
            acc[t] += dot(bmat[chip], pair(gall, t, chip, 4), (0, 0))

    def forward(step):
        from_sibling(1, hall, step)
        for t in range(2):
            chip = origin(t, step)
            more = dot(fmat[chip], pair(hall, t, chip, 3), (1, 0))
            hacc[t] = more if step == 0 else hacc[t] + more

    backward(0)
    done = 1
    for step in range(3, Z):
        ring(0, gall, step)
        while done < step:
            backward(done)
            done += 1
    ring(1, hall, 0)
    while done < Z:
        backward(done)
        done += 1

    one = Reduction(p, part, 0, factor, big, (big_send, big_recv), sends)
    two = Reduction(p, part, 5, factor, small, (small_send, small_recv), sends)

    for t in range(2):
        actcot[t, :, :256] = (acc[t] * f1[t]).astype(BF16)
        actcot[t, :, 256:] = (acc[t] * f2[t]).astype(BF16)
    ring(1, hall, 1)
    second = dot(x_ref[0], actcot[1], (0, 0))
    part[1] = second[:, :256]
    part[3] = second[:, 256:]
    first = dot(x_ref[0], actcot[0], (0, 0)) + dot(x_ref[1], actcot[1], (0, 0))
    part[0] = first[:, :256]
    part[2] = first[:, 256:]
    one.start_core()
    forward(0)
    if Z > 2:
        ring(1, hall, 2)
    for t in range(2):
        total = cot_ref[t].astype(F32)
        for tap in range(2 - t):
            a = actcot[t + tap]
            total = total + dot(a[:, :256], wf[tap], (1, 1)) + dot(a[:, 256:], wg[tap], (1, 1))
        gi_ref[t] = total.astype(BF16)
    one.start_y()
    done = 1
    stages = {5: one.start_x, 6: one.start_z}
    for step in range(3, Z):
        ring(1, hall, step)
        while done < step:
            forward(done)
            done += 1
        if step in stages:
            stages.pop(step)()
    while done < Z:
        forward(done)
        done += 1
    for t in range(2):
        here = dot(hacc[t].astype(BF16), cot_ref[t], (0, 0))
        part[5] = here if t == 0 else part[5] + here
    two.start_core()
    for stage in stages.values():
        stage()
    one.start_gather_x()
    two.start_y()
    one.start_gather_y()
    two.start_x()
    two.start_z()
    two.start_gather_x()
    one.start_gather_core()
    two.start_gather_y()
    two.start_gather_core()
    one.finish([(gf_ref, 0), (gf_ref, 1), (gg_ref, 0), (gg_ref, 1), (gm_ref, 0)])
    two.finish([(gm_ref, 1)])
    for item in sends:
        item.wait_send()


def reduction_scratch(count, chans, Y, Z):
    rows = TILE // Y
    return [
        pltpu.VMEM((count, TILE, chans), F32),
        pltpu.VMEM((Y, count, rows, chans), BF16),
        pltpu.VMEM((Y - 1, count, rows, chans), BF16),
        pltpu.VMEM((X, count, rows // 2, 128), F32),
        pltpu.VMEM((X - 1, count, rows // 2, 128), F32),
        pltpu.VMEM((Z, count, rows // 2, 128), F32),
        pltpu.VMEM((X, count, rows // 2, 128), F32),
        pltpu.VMEM((Y, count, rows, chans), BF16),
        pltpu.VMEM((Y, count, rows, chans), BF16),
    ]


def solution(mesh):
    Y, Z = mesh.shape["dp"] // X, mesh.shape["region"] // 2
    R = 2 * Z

    def per_device(inputs, cotangent, w_filter, w_gate, w_mix, neighbours, adjacency):
        _, steps, sites, chans = inputs.shape
        total_rows = steps * sites * mesh.shape["dp"] * R
        per_tile = neighbours.shape[1]
        dma = pltpu.SemaphoreType.DMA
        stages = 2 * Y + 2 * X + Z + 1
        vmem = pl.BlockSpec(memory_space=pltpu.VMEM)
        grads = jax.ShapeDtypeStruct((2, chans, chans), F32)
        grad_inputs, grad_filter, grad_gate, grad_mix = pl.pallas_call(
            functools.partial(kernel, Y, Z, 1.0 / math.sqrt(total_rows)),
            out_shape=(jax.ShapeDtypeStruct((steps, sites, chans), BF16), grads, grads, grads),
            in_specs=[pl.BlockSpec(memory_space=pltpu.SMEM)] + [vmem] * 6,
            out_specs=(vmem,) * 4,
            scratch_shapes=[
                pltpu.VMEM((2, R, 2, TILE, chans), BF16),
                pltpu.VMEM((2, R, 2, TILE, chans), BF16),
                pltpu.VMEM((R, TILE // Y, TILE), BF16),
                pltpu.VMEM((R, TILE // Y, TILE), BF16),
                pltpu.VMEM((Y, R, TILE // Y, TILE), BF16),
                pltpu.VMEM((Z, 2 * TILE, 2 * TILE), BF16),
                pltpu.VMEM((Z, 2 * TILE, 2 * TILE), BF16),
                pltpu.VMEM((2, sites, chans), F32),
                pltpu.VMEM((2, sites, chans), F32),
                pltpu.VMEM((2, sites, chans), F32),
                pltpu.VMEM((2, sites, chans), F32),
                pltpu.VMEM((2, sites, 2 * chans), BF16),
                pltpu.VMEM((6, chans, chans), F32),
                pltpu.SMEM((6, R), jnp.int32),
                *reduction_scratch(5, chans, Y, Z),
                *reduction_scratch(1, chans, Y, Z),
                dma((2, 2, Z, 2)), dma((2, 2, Z, 2)),
                dma((2, 2, Z, 2)), dma((2, 2, Z, 2)),
                dma((R + Y,)), dma((R + Y,)),
                dma((stages,)), dma((stages,)),
                dma((stages,)), dma((stages,)),
            ],
            compiler_params=pltpu.CompilerParams(
                collective_id=0, has_side_effects=True, vmem_limit_bytes=48 << 20),
            name="train_step",
        )(neighbours, inputs[0], cotangent[0], w_filter, w_gate, w_mix,
          adjacency.reshape(2 * per_tile, TILE, TILE))
        return grad_inputs[None], grad_filter, grad_gate, grad_mix

    return jax.shard_map(
        per_device,
        mesh=mesh,
        in_specs=(
            P("dp", None, "region", None),
            P("dp", None, "region", None),
            P(),
            P(),
            P(),
            P(),
            P("region", None, None, None),
        ),
        out_specs=(P("dp", None, "region", None), P(), P(), P()),
        check_vma=False,
    )
```

time: 430 us -> 125 us (0.29)
  waiting for transfers between devices: 363 us -> 0 us
  Pallas kernels: 0 us -> 114 us
  matrix products: 15.4 us -> 0 us
  between operations: 14.3 us -> 0.66 us
  starting transfers between devices: 12 us -> 0 us
  local copies, waits for them, and re-layouts: 17 us -> 9.59 us
  other arithmetic: 6.99 us -> 0 us
    psum x1 -> x0, waiting for transfers between devices: 274 us -> none  [per_device(): conv_total, mix_total = lax.psum((conv_sum, mix_sum), ('dp', 'region'))]
    pallas_call x0 -> x1, Pallas kernels: none -> 114 us  [per_device(): pl.pallas_call(functools.partial(kernel, Y, Z, 1.0 / math.sqrt(total_rows...]
    all_to_all x1 -> x0, waiting for transfers between devices: 46.4 us -> none  [per_device(): lax.all_to_all(outgoing_back, 'region', split_axis=2, concat_axis=2, tile...]
    all_gather x1 -> x0, waiting for transfers between devices: 42.7 us -> none  [per_device(): piece = lax.all_gather(tiled, 'region', axis=2, tiled=True)]
    dot_general x10 -> x0, matrix products: 15.4 us -> none  [the longest x1 4.67 us: per_device(): jnp.einsum('en,btnqc->bteqc', select, piece, preferred_element_type=jnp.f...]
    all_to_all x1 -> x0, starting transfers between devices: 11.9 us -> none  [per_device(): lax.all_to_all(outgoing_back, 'region', split_axis=2, concat_axis=2, tile...]
    unnamed x37 -> x19, local copies, waits for them, and re-layouts: 3.64 us -> 9.59 us
    scatter x1 -> x0, local copies, waits for them, and re-layouts: 5.34 us -> none  [per_device(): outgoing_back = outgoing_back.at[:, :, drop_index].set(term, mode='drop')]
  transfers between devices with their start and end apart: 3 -> 0, of which waited for: 3 -> 0; matrix products, arithmetic and copies ran while one was open for 1% -> 0% of each run, Pallas kernels for 0% -> 0%
where the time goes in v1:
time: 125 us; the launch traced here: 124 us
  Pallas kernels  114 us (91%)
  local copies, waits for them, and re-layouts  9.59 us (8%)
    pallas_call x1, Pallas kernels, per_device(): pl.pallas_call(functools.partial(kernel, Y, Z, 1.0 / math.sqrt(total_rows...  114 us
    unnamed x19, local copies, waits for them, and re-layouts  9.59 us

profile of v1, /device:TPU:1, one launch (start us, length us, event | category | flops | bytes accessed | tf_op | source)
XLA Modules:
  0.0 124.4 jit_solution(10752418720693866596)
XLA Ops:
  0.6 0.0 copy-start.6
  0.6 0.7 copy-done.6
  1.3 0.1 copy.11.nbr
  1.4 0.0 copy-start
  1.4 1.0 copy-done
  2.4 0.0 copy-start.1
  2.4 0.9 copy-done.1
  3.4 0.0 copy-start.2
  3.4 0.9 copy-done.2
  4.3 0.0 copy-start.3
  4.3 0.9 copy-done.3
  5.3 0.0 copy-start.4
  5.3 0.9 copy-done.4
  6.2 0.0 copy-start.5
  6.2 0.9 copy-done.5
  7.2 114.2 %train_step.1 = (bf16[2,256,256]{2,1,0:T(8,128)(2,1)S(1)}, f32[2,256,256]{2,1,0:T(8,128)S(1)}, f32[2,256,256]{2,1,0:T(8,128)S(1)}, f32[2,256,256]{2,1,0:T(8,128)S(1)}) custom-call(s32[32,6]{1,0:T(8,128)S(1)} %copy.11.nbr, bf16[2,256,256]{2,1,0:T(8,128)(2,1)S(1)} %bitcast.6, bf16[2,256,256]{2,1,0:T(8,128)(2,1)S(1)} %bitcast.7, ...), custom_call_target="tpu_custom_call" | custom-call | tf_op jit(solution)/shard_map/train_step/pallas_call | solution.py:404
  121.3 0.7 copy.16
  122.0 0.8 copy.17
  122.8 0.8 copy.18
  123.6 0.8 copy.19
Async XLA Ops:
  0.6 0.7 copy-start.6
  1.4 1.0 copy-start
  2.4 0.9 copy-start.1
  3.4 0.9 copy-start.2
  4.3 0.9 copy-start.3
  5.3 0.9 copy-start.4
  6.2 0.9 copy-start.5

commit v2 on v0

v2 whole, which is shorter than its diff:
```python
import functools
import math

import jax
import jax.numpy as jnp
from jax import lax
from jax.experimental import pallas as pl
from jax.experimental.pallas import tpu as pltpu
from jax.sharding import PartitionSpec as P

MESH = pl.DeviceIdType.MESH
X = 4
TILE = 128
CHUNKS = 4
ORDERS = ("yxz", "zyx", "xzy")
F32 = jnp.float32
BF16 = jnp.bfloat16


def dot(a, b, contract):
    return lax.dot_general(a, b, ((contract[:1], contract[1:]), ((), ())), preferred_element_type=F32)


class Place:
    def __init__(self, Y, Z):
        self.size = {"x": X, "y": Y, "z": Z}
        self.dp = lax.axis_index("dp")
        self.region = lax.axis_index("region")
        self.at = {
            "x": lax.div(self.dp, Y), "y": lax.rem(self.dp, Y), "z": lax.div(self.region, 2),
        }
        self.c = lax.rem(self.region, 2)
        self.sibling = (self.dp, self.at["z"] * 2 + 1 - self.c)

    def along(self, axis, i):
        at = dict(self.at)
        at[axis] = lax.rem(at[axis] + i, self.size[axis])
        return (at["x"] * self.size["y"] + at["y"], at["z"] * 2 + self.c)


class Reduction:
    def __init__(self, place, order, part, base, factor, scratch, sems, sends):
        self.p, self.order, self.part, self.base, self.factor, self.sends = place, order, part, base, factor, sends
        self.core, self.s1, self.r1, self.s2, self.r2, self.x3, self.g2, self.g1, self.cg = scratch
        self.send, self.recv = sems
        self.items, self.used = [], 0

    def copy(self, src, dst, device):
        item = pltpu.make_async_remote_copy(
            src_ref=src, dst_ref=dst, send_sem=self.send.at[self.used], recv_sem=self.recv.at[self.used],
            device_id=device, device_id_type=MESH,
        )
        self.used += 1
        item.start()
        self.sends.append(item)
        self.items.append(item)

    def wait(self):
        for item in self.items:
            item.wait_recv()
        self.items = []

    def peers(self, k):
        axis = self.order[k]
        n, at = self.p.size[axis], self.p.at[axis]
        return n, at, [(i, lax.rem(at + i, n), self.p.along(axis, i)) for i in range(1, n)]

    def start_core(self):
        other = pl.ds(pl.multiple_of((1 - self.p.c) * TILE, TILE), TILE)
        self.copy(self.part.at[pl.ds(self.base, 2), other], self.core, self.p.sibling)

    def start_first(self):
        self.wait()
        n, at, peers = self.peers(0)
        mine = pl.ds(pl.multiple_of(self.p.c * TILE, TILE), TILE)
        for i in range(2):
            total = self.core[i] + self.part[self.base + i, mine]
            self.core[i] = total
            self.s1[:, i] = total.astype(BF16).reshape(n, TILE // n, total.shape[-1])
        for i, slot, device in peers:
            self.copy(self.s1.at[slot], self.r1.at[i - 1], device)

    def start_second(self):
        self.wait()
        first, at, _ = self.peers(0)
        rows = TILE // first
        tiles = []
        for i in range(2):
            total = self.core[i, pl.ds(pl.multiple_of(at * rows, rows), rows)]
            for j in range(first - 1):
                total = total + self.r1[j, i].astype(F32)
            tiles += [
                total[r * 8:r * 8 + 8, h * 128:h * 128 + 128] for r in range(rows // 8) for h in range(2)
            ]
        n, at, peers = self.peers(1)
        each = len(tiles) // n
        for index, tile in enumerate(tiles):
            self.s2[index // each, index % each] = tile
        for i, slot, device in peers:
            self.copy(self.s2.at[slot], self.r2.at[i - 1], device)

    def start_third(self):
        self.wait()
        n, at, _ = self.peers(1)
        total = self.s2[at]
        for j in range(n - 1):
            total = total + self.r2[j]
        n, at, peers = self.peers(2)
        self.x3[at] = total
        for i, slot, device in peers:
            self.copy(self.x3.at[at], self.x3.at[at], device)

    def start_gather_second(self):
        self.wait()
        total = self.x3[0]
        for j in range(1, self.peers(2)[0]):
            total = total + self.x3[j]
        n, at, peers = self.peers(1)
        self.g2[at] = total * self.factor
        for i, slot, device in peers:
            self.copy(self.g2.at[at], self.g2.at[at], device)

    def start_gather_first(self):
        self.wait()
        n, at, peers = self.peers(0)
        each = self.g2.shape[1]
        tiles = [self.g2[i, j] for i in range(self.g2.shape[0]) for j in range(each)]
        for i in range(2):
            mine = tiles[i * len(tiles) // 2:(i + 1) * len(tiles) // 2]
            rows = [jnp.concatenate(mine[r:r + 2], axis=1) for r in range(0, len(mine), 2)]
            self.g1[at, i] = jnp.concatenate(rows, axis=0).astype(BF16)
        for i, slot, device in peers:
            self.copy(self.g1.at[at], self.g1.at[at], device)

    def start_gather_core(self):
        self.wait()
        self.copy(self.g1, self.cg, self.p.sibling)

    def finish(self, out):
        for source, core in ((self.g1, self.p.c), (self.cg, 1 - self.p.c)):
            if source is self.cg:
                self.wait()
            rows = pl.ds(pl.multiple_of(core * TILE, TILE), TILE)
            for i in range(2):
                out[self.base + i, rows] = source[:, i].reshape(TILE, out.shape[-1]).astype(F32)


def kernel(Y, Z, factor, nbr, x_hbm, cot_hbm, wf_hbm, wg_hbm, wm_hbm, adj_hbm,
           gi_ref, out_ref,
           x_ref, wf, wg, wm, adj, gall, asend, arecv, afull, bmat, direct, acc, hid, f1, f2, actcot, part, table,
           *rest):
    scratch = [rest[9 * i:9 * i + 9] for i in range(3)]
    local_sem, ring_send, ring_recv, sib_send, sib_recv, adj_send, adj_recv = rest[27:34]
    sems = [rest[34 + 2 * i:36 + 2 * i] for i in range(3)]
    p = Place(Y, Z)
    R = 2 * Z
    per_tile = nbr.shape[0]
    entries = 2 * per_tile
    rows = TILE // Y
    sends = []

    def fetch(i, src, dst):
        item = pltpu.make_async_copy(src, dst, local_sem.at[i])
        item.start()
        return item

    get_cot = [fetch(t, cot_hbm.at[t], gall.at[t, p.region]) for t in range(2)]
    get_adj = fetch(2, adj_hbm, adj)
    get_x = fetch(3, x_hbm, x_ref)
    get_wf = fetch(4, wf_hbm, wf)
    get_wg = fetch(5, wg_hbm, wg)
    get_wm = fetch(6, wm_hbm, wm)

    barrier = pltpu.get_barrier_semaphore()
    partners = [(p.dp, lax.rem(p.region + i, R)) for i in range(1, R)]
    partners += [p.along(axis, i) for axis, n in (("x", X), ("y", Y)) for i in range(1, n)]
    for device in partners:
        pl.semaphore_signal(barrier, inc=1, device_id=device, device_id_type=MESH)

    def remote(src, dst, send, recv, device):
        item = pltpu.make_async_remote_copy(
            src_ref=src, dst_ref=dst, send_sem=send, recv_sem=recv, device_id=device, device_id_type=MESH)
        item.start()
        sends.append(item)

    def arrived(ref, send, recv):
        pltpu.make_async_remote_copy(
            src_ref=ref, dst_ref=ref, send_sem=send, recv_sem=recv, device_id=p.sibling, device_id_type=MESH
        ).wait_recv()

    def origin(direction, step):
        return lax.rem(p.at["z"] + (Z - step if direction == 0 else step), Z)

    piece = 2 * TILE // CHUNKS

    def ring(step):
        for chunk in range(CHUNKS):
            for direction in range(2):
                block = gall.at[direction, origin(direction, step) * 2 + p.c, pl.ds(chunk * piece, piece)]
                if step > 0:
                    arrived(block, ring_send.at[direction, step - 1, chunk], ring_recv.at[direction, step - 1, chunk])
                if step < Z - 1:
                    remote(block, block, ring_send.at[direction, step, chunk], ring_recv.at[direction, step, chunk],
                           p.along("z", 1 if direction == 0 else Z - 1))
        for direction in range(2):
            block = gall.at[direction, origin(direction, step) * 2 + p.c]
            remote(block, block, sib_send.at[direction, step], sib_recv.at[direction, step], p.sibling)

    def scan(region, carry):
        entry = valid = other = mine = jnp.int32(0)
        for e in range(entries):
            a = nbr[e % per_tile, p.region * 2 + e // per_tile]
            hit = lax.div(a, 2) == region
            entry = jnp.where(hit, e, entry)
            valid = jnp.where(hit, 1, valid)
            b = nbr[e % per_tile, region * 2 + e // per_tile]
            back = lax.div(b, 2) == p.region
            other = jnp.where(back, e // per_tile, other)
            mine = jnp.where(back, lax.rem(b, 2), mine)
        for row, value in enumerate((entry, valid, other, mine)):
            table[row, region] = value
        return carry

    def fill(region, carry):
        block = adj[table[0, region], pl.ds(pl.multiple_of(p.at["y"] * rows, rows), rows)]
        asend[region] = jnp.where(table[1, region] == 1, block, jnp.zeros_like(block))
        return carry

    def forward(t):
        pre_f = dot(x_ref[t], wf[0], (1, 0))
        pre_g = dot(x_ref[t], wg[0], (1, 0))
        if t == 1:
            pre_f = pre_f + dot(x_ref[0], wf[1], (1, 0))
            pre_g = pre_g + dot(x_ref[0], wg[1], (1, 0))
        filt = jnp.tanh(pre_f)
        gate = jax.nn.sigmoid(pre_g)
        both = filt * gate
        hid[t] = both.astype(BF16)
        f1[t] = gate * (1.0 - filt * filt)
        f2[t] = both * (1.0 - gate)

    def own_products():
        for t in range(2):
            cot = gall[t, p.region]
            direct[t] = dot(cot, wm[0], (1, 1))
            here = dot(hid[t], cot, (0, 0))
            part[0] = here if t == 0 else part[0] + here

    def send_adjacency():
        arecv[p.region] = asend[p.region]
        for i in range(1, R):
            target = lax.rem(p.region + i, R)
            remote(asend.at[target], arecv.at[p.region], adj_send.at[i], adj_recv.at[i], (p.dp, target))

    def share_adjacency():
        for i in range(1, R):
            source = lax.rem(p.region + R - i, R)
            arrived(arecv.at[source], adj_send.at[i], adj_recv.at[i])
        for i in range(1, Y):
            remote(arecv, afull.at[p.at["y"]], adj_send.at[R + i], adj_recv.at[R + i], p.along("y", i))
        afull[p.at["y"]] = arecv[...]

    def wait_adjacency():
        for i in range(1, Y):
            source = lax.rem(p.at["y"] + Y - i, Y)
            arrived(afull.at[source], adj_send.at[R + i], adj_recv.at[R + i])

    def build(chip, carry):
        for core in range(2):
            region = chip * 2 + core
            block = afull[:, region].reshape(TILE, TILE).T
            zero = jnp.zeros_like(block)
            for j in range(2):
                bmat[chip, j * TILE:(j + 1) * TILE, core * TILE:(core + 1) * TILE] = jnp.where(
                    table[3, region] == j, block, zero)
        return carry

    def gathered(step):
        for direction in range(2):
            block = gall.at[direction, origin(direction, step) * 2 + 1 - p.c]
            arrived(block, sib_send.at[direction, step], sib_recv.at[direction, step])
        for t in range(2):
            chip = origin(t, step)
            halves = []
            for core in range(2):
                region = chip * 2 + core
                halves.append(jnp.where(table[2, region] == 0, gall[t, region, :TILE], gall[t, region, TILE:]))
            more = dot(bmat[chip], jnp.concatenate(halves, axis=0), (1, 0))
            acc[t] = more if step == 0 else acc[t] + more

    for item in get_cot:
        item.wait()
    pl.semaphore_wait(barrier, len(partners))
    ring(0)
    lax.fori_loop(0, R, scan, 0)
    get_adj.wait()
    lax.fori_loop(0, R, fill, 0)
    send_adjacency()
    ring(1)
    for item in (get_x, get_wf, get_wg):
        item.wait()
    forward(0)
    ring(2)
    share_adjacency()
    forward(1)
    get_wm.wait()
    ring(3)
    own_products()
    work = [wait_adjacency, lambda: lax.fori_loop(0, Z, build, 0)]
    work += [functools.partial(gathered, step) for step in range(Z - 1)]
    per_step = -(-len(work) // max(1, Z - 4))
    for step in range(4, Z):
        ring(step)
        for item in work[:per_step]:
            item()
        work = work[per_step:]
    for item in work:
        item()
    gathered(Z - 1)

    groups = [
        Reduction(p, order, part, 2 * i, factor, scratch[i], sems[i], sends) for i, order in enumerate(ORDERS)
    ]
    mixed = [acc[t].astype(BF16) for t in range(2)]
    part[1] = dot(hid[0], mixed[0], (0, 0)) + dot(hid[1], mixed[1], (0, 0))
    groups[0].start_core()
    for t in range(2):
        grad = direct[t] + dot(mixed[t], wm[1], (1, 1))
        actcot[0, t] = (grad * f1[t]).astype(BF16)
        actcot[1, t] = (grad * f2[t]).astype(BF16)
    for g in range(2):
        part[2 + 2 * g] = dot(x_ref[0], actcot[g, 0], (0, 0)) + dot(x_ref[1], actcot[g, 1], (0, 0))
        part[3 + 2 * g] = dot(x_ref[0], actcot[g, 1], (0, 0))
        groups[1 + g].start_core()
    for group in groups:
        group.start_first()
    for t in range(2):
        total = gall[t, p.region].astype(F32)
        for tap in range(2 - t):
            total = total + dot(actcot[0, t + tap], wf[tap], (1, 1)) + dot(actcot[1, t + tap], wg[tap], (1, 1))
        gi_ref[t] = total.astype(BF16)
    for stage in ("start_second", "start_third", "start_gather_second", "start_gather_first", "start_gather_core"):
        for group in groups:
            getattr(group, stage)()
    for group in groups:
        group.finish(out_ref)
    for item in sends:
        item.wait_send()


def write(gi, grads, gi_out, gf_out, gg_out, gm_out, sem):
    copies = [
        pltpu.make_async_copy(gi, gi_out, sem.at[0]),
        pltpu.make_async_copy(grads.at[pl.ds(0, 2)], gm_out, sem.at[1]),
        pltpu.make_async_copy(grads.at[pl.ds(2, 2)], gf_out, sem.at[2]),
        pltpu.make_async_copy(grads.at[pl.ds(4, 2)], gg_out, sem.at[3]),
    ]
    for item in copies:
        item.start()
    for item in copies:
        item.wait()


def reduction_scratch(order, chans, sizes):
    n1, n2, n3 = (sizes[axis] for axis in order)
    each = 2 * (TILE // n1 // 8) * (chans // 128) // n2
    return [
        pltpu.VMEM((2, TILE, chans), F32),
        pltpu.VMEM((n1, 2, TILE // n1, chans), BF16),
        pltpu.VMEM((n1 - 1, 2, TILE // n1, chans), BF16),
        pltpu.VMEM((n2, each, 8, 128), F32),
        pltpu.VMEM((n2 - 1, each, 8, 128), F32),
        pltpu.VMEM((n3, each, 8, 128), F32),
        pltpu.VMEM((n2, each, 8, 128), F32),
        pltpu.VMEM((n1, 2, TILE // n1, chans), BF16),
        pltpu.VMEM((n1, 2, TILE // n1, chans), BF16),
    ]


def solution(mesh):
    Y, Z = mesh.shape["dp"] // X, mesh.shape["region"] // 2
    R = 2 * Z
    sizes = {"x": X, "y": Y, "z": Z}

    def per_device(inputs, cotangent, w_filter, w_gate, w_mix, neighbours, adjacency):
        _, steps, sites, chans = inputs.shape
        total_rows = steps * sites * mesh.shape["dp"] * R
        per_tile = neighbours.shape[1]
        dma = pltpu.SemaphoreType.DMA
        vmem = pl.BlockSpec(memory_space=pltpu.VMEM)
        hbm = pl.BlockSpec(memory_space=pltpu.HBM)
        scratch, sems = [], []
        for order in ORDERS:
            scratch += reduction_scratch(order, chans, sizes)
            n1, n2, n3 = (sizes[axis] for axis in order)
            count = 2 + 2 * (n1 - 1) + 2 * (n2 - 1) + n3 - 1
            sems += [dma((count,)), dma((count,))]
        weights = pltpu.VMEM((2, chans, chans), BF16)
        wide = pltpu.VMEM((steps, sites, chans), F32)
        narrow = pltpu.VMEM((steps, sites, chans), BF16)
        grad_inputs, grads = pl.pallas_call(
            functools.partial(kernel, Y, Z, 1.0 / math.sqrt(total_rows)),
            out_shape=(
                jax.ShapeDtypeStruct((steps, sites, chans), BF16), jax.ShapeDtypeStruct((6, chans, chans), F32),
            ),
            in_specs=[pl.BlockSpec(memory_space=pltpu.SMEM)] + [hbm] * 6,
            out_specs=(vmem, vmem),
            scratch_shapes=[
                narrow, weights, weights, weights,
                pltpu.VMEM((2 * per_tile, TILE, TILE), BF16),
                pltpu.VMEM((steps, R, sites, chans), BF16),
                pltpu.VMEM((R, TILE // Y, TILE), BF16),
                pltpu.VMEM((R, TILE // Y, TILE), BF16),
                pltpu.VMEM((Y, R, TILE // Y, TILE), BF16),
                pltpu.VMEM((Z, 2 * TILE, 2 * TILE), BF16),
                wide, wide, narrow, wide, wide,
                pltpu.VMEM((2, steps, sites, chans), BF16),
                pltpu.VMEM((6, chans, chans), F32),
                pltpu.SMEM((4, R), jnp.int32),
                *scratch,
                dma((7,)),
                dma((2, Z, CHUNKS)), dma((2, Z, CHUNKS)),
                dma((2, Z)), dma((2, Z)),
                dma((R + Y,)), dma((R + Y,)),
                *sems,
            ],
            compiler_params=pltpu.CompilerParams(
                collective_id=0, has_side_effects=True, vmem_limit_bytes=56 << 20),
            name="train_step",
        )(neighbours.T, inputs[0], cotangent[0], w_filter, w_gate, w_mix,
          adjacency.reshape(2 * per_tile, TILE, TILE))
        grad = jax.ShapeDtypeStruct((2, chans, chans), F32)
        grad_inputs, grad_filter, grad_gate, grad_mix = pl.pallas_call(
            write,
            out_shape=(jax.ShapeDtypeStruct((steps, sites, chans), BF16), grad, grad, grad),
            in_specs=[pl.BlockSpec(memory_space=pl.ANY)] * 2,
            out_specs=(hbm,) * 4,
            scratch_shapes=[dma((4,))],
            name="write",
        )(grad_inputs, grads)
        return grad_inputs[None], grad_filter, grad_gate, grad_mix

    return jax.shard_map(
        per_device,
        mesh=mesh,
        in_specs=(
            P("dp", None, "region", None),
            P("dp", None, "region", None),
            P(),
            P(),
            P(),
            P(),
            P("region", None, None, None),
        ),
        out_specs=(P("dp", None, "region", None), P(), P(), P()),
        check_vma=False,
    )
```

time: 430 us -> 143 us (0.33)
  waiting for transfers between devices: 363 us -> 0 us
  Pallas kernels: 0 us -> 143 us
  local copies, waits for them, and re-layouts: 17 us -> 0 us
  matrix products: 15.4 us -> 0 us
  between operations: 14.3 us -> 0.64 us
  starting transfers between devices: 12 us -> 0 us
  other arithmetic: 6.99 us -> 0 us
    psum x1 -> x0, waiting for transfers between devices: 274 us -> none  [per_device(): conv_total, mix_total = lax.psum((conv_sum, mix_sum), ('dp', 'region'))]
    pallas_call x0 -> x2, Pallas kernels: none -> 143 us  [the longest x1 85.9 us: per_device(): pl.pallas_call(functools.partial(kernel, Y, Z, 1.0 / math.sqrt(total_rows...]
    all_to_all x1 -> x0, waiting for transfers between devices: 46.4 us -> none  [per_device(): lax.all_to_all(outgoing_back, 'region', split_axis=2, concat_axis=2, tile...]
    all_gather x1 -> x0, waiting for transfers between devices: 42.7 us -> none  [per_device(): piece = lax.all_gather(tiled, 'region', axis=2, tiled=True)]
    dot_general x10 -> x0, matrix products: 15.4 us -> none  [the longest x1 4.67 us: per_device(): jnp.einsum('en,btnqc->bteqc', select, piece, preferred_element_type=jnp.f...]
    all_to_all x1 -> x0, starting transfers between devices: 11.9 us -> none  [per_device(): lax.all_to_all(outgoing_back, 'region', split_axis=2, concat_axis=2, tile...]
    scatter x1 -> x0, local copies, waits for them, and re-layouts: 5.34 us -> none  [per_device(): outgoing_back = outgoing_back.at[:, :, drop_index].set(term, mode='drop')]
    reshape x7 -> x0, local copies, waits for them, and re-layouts: 4.3 us -> none  [the longest x1 3.13 us: per_device(): outgoing_back.reshape(windows, steps, regions, capacity, 128, chans)]
  transfers between devices with their start and end apart: 3 -> 0, of which waited for: 3 -> 0; matrix products, arithmetic and copies ran while one was open for 1% -> 0% of each run, Pallas kernels for 0% -> 0%
where the time goes in v2:
time: 143 us
  Pallas kernels  143 us (100%)
    pallas_call x1, Pallas kernels, per_device(): pl.pallas_call(functools.partial(kernel, Y, Z, 1.0 / math.sqrt(total_rows...  85.9 us
    pallas_call x1, Pallas kernels, per_device(): pl.pallas_call(write, out_shape=(jax.ShapeDtypeStruct((steps, sites, chan...  56.7 us

profile of v2, /device:TPU:1, one launch (start us, length us, event | category | flops | bytes accessed | tf_op | source)
XLA Modules:
  0.0 143.3 jit_solution(2249123616865882470)
XLA Ops:
  0.6 85.9 %train_step.1 = (bf16[2,256,256]{2,1,0:T(8,128)(2,1)}, f32[6,256,256]{2,1,0:T(8,128)}) custom-call(s32[6,32]{1,0:T(8,128)} %bitcast.8, bf16[2,256,256]{2,1,0:T(8,128)(2,1)} %bitcast.6, bf16[2,256,256]{2,1,0:T(8,128)(2,1)} %bitcast.7, bf16[2,256,256]{2,1,0:T(8,128)(2,1)} %wf_hbm.1, bf16[2,256,256]{2,1,0:T(8,128)(2,1)} %wg_hbm.1, bf16[2,256,256]{2,1,0:T(8,128)(2,1)} %wm_hbm.1, ...), custom_call_target="tpu_custom_call" | custom-call | tf_op jit(solution)/shard_map/train_step/pallas_call | solution.py:401
  86.6 56.7 %write.1 = (bf16[2,256,256]{2,1,0:T(8,128)(2,1)}, f32[2,256,256]{2,1,0:T(8,128)}, f32[2,256,256]{2,1,0:T(8,128)}, f32[2,256,256]{2,1,0:T(8,128)}) custom-call(bf16[2,256,256]{2,1,0:T(8,128)(2,1)} %get-tuple-element.10.gi, f32[6,256,256]{2,1,0:T(8,128)} %get-tuple-element.11.grads), custom_call_target="tpu_custom_call" | custom-call | tf_op jit(solution)/shard_map/write/pallas_call | solution.py:433

commit v3 on v2

--- a/solution.py
+++ b/solution.py
@@ -11,8 +11,7 @@
 MESH = pl.DeviceIdType.MESH
 X = 4
 TILE = 128
-CHUNKS = 4
-ORDERS = ("yxz", "zyx", "xzy")
+ORDERS = ("yxz", "zxy", "xzy")
 F32 = jnp.float32
 BF16 = jnp.bfloat16
 
@@ -136,18 +135,19 @@
         self.wait()
         self.copy(self.g1, self.cg, self.p.sibling)
 
-    def finish(self, out):
-        for source, core in ((self.g1, self.p.c), (self.cg, 1 - self.p.c)):
-            if source is self.cg:
-                self.wait()
-            rows = pl.ds(pl.multiple_of(core * TILE, TILE), TILE)
-            for i in range(2):
-                out[self.base + i, rows] = source[:, i].reshape(TILE, out.shape[-1]).astype(F32)
+    def put(self, out, sem, other):
+        source, core = (self.cg, 1 - self.p.c) if other else (self.g1, self.p.c)
+        copies = [
+            pltpu.make_async_copy(source.at[:, i], out.at[i, core], sem.at[other, self.base + i]) for i in range(2)
+        ]
+        for item in copies:
+            item.start()
+        return copies
 
 
 def kernel(Y, Z, factor, nbr, x_hbm, cot_hbm, wf_hbm, wg_hbm, wm_hbm, adj_hbm,
-           gi_ref, out_ref,
-           x_ref, wf, wg, wm, adj, gall, asend, arecv, afull, bmat, direct, acc, hid, f1, f2, actcot, part, table,
+           gi_ref, out_mix, out_filter, out_gate,
+           gi_vmem, put_sem, x_ref, wf, wg, wm, adj, gall, asend, arecv, afull, bmat, direct, acc, hid, f1, f2, actcot, part, table,
            *rest):
     scratch = [rest[9 * i:9 * i + 9] for i in range(3)]
     local_sem, ring_send, ring_recv, sib_send, sib_recv, adj_send, adj_recv = rest[27:34]
@@ -156,7 +156,7 @@
     R = 2 * Z
     per_tile = nbr.shape[0]
     entries = 2 * per_tile
-    rows = TILE // Y
+    rows = TILE // X
     sends = []
 
     def fetch(i, src, dst):
@@ -191,20 +191,24 @@
     def origin(direction, step):
         return lax.rem(p.at["z"] + (Z - step if direction == 0 else step), Z)
 
-    piece = 2 * TILE // CHUNKS
-
     def ring(step):
-        for chunk in range(CHUNKS):
+        for t in range(2):
             for direction in range(2):
-                block = gall.at[direction, origin(direction, step) * 2 + p.c, pl.ds(chunk * piece, piece)]
-                if step > 0:
-                    arrived(block, ring_send.at[direction, step - 1, chunk], ring_recv.at[direction, step - 1, chunk])
-                if step < Z - 1:
-                    remote(block, block, ring_send.at[direction, step, chunk], ring_recv.at[direction, step, chunk],
-                           p.along("z", 1 if direction == 0 else Z - 1))
-        for direction in range(2):
-            block = gall.at[direction, origin(direction, step) * 2 + p.c]
-            remote(block, block, sib_send.at[direction, step], sib_recv.at[direction, step], p.sibling)
+                reach = Z // 2 if t == direction else Z // 2 - 1
+                if step > reach:
+                    continue
+                slot = origin(direction, step) * 2 + p.c
+                for tile in range(2):
+                    block = gall.at[t, slot, pl.ds(tile * TILE, TILE)]
+                    if step > 0:
+                        arrived(block, ring_send.at[direction, t, step - 1, tile],
+                                ring_recv.at[direction, t, step - 1, tile])
+                    if step < reach:
+                        remote(block, block, ring_send.at[direction, t, step, tile],
+                               ring_recv.at[direction, t, step, tile], p.along("z", 1 if direction == 0 else Z - 1))
+                if step > 0 or direction == 0:
+                    block = gall.at[t, slot]
+                    remote(block, block, sib_send.at[direction, t, step], sib_recv.at[direction, t, step], p.sibling)
 
     def scan(region, carry):
         entry = valid = other = mine = jnp.int32(0)
@@ -222,7 +226,7 @@
         return carry
 
     def fill(region, carry):
-        block = adj[table[0, region], pl.ds(pl.multiple_of(p.at["y"] * rows, rows), rows)]
+        block = adj[table[0, region], pl.ds(pl.multiple_of(p.at["x"] * rows, rows), rows)]
         asend[region] = jnp.where(table[1, region] == 1, block, jnp.zeros_like(block))
         return carry
 
@@ -256,13 +260,13 @@
         for i in range(1, R):
             source = lax.rem(p.region + R - i, R)
             arrived(arecv.at[source], adj_send.at[i], adj_recv.at[i])
-        for i in range(1, Y):
-            remote(arecv, afull.at[p.at["y"]], adj_send.at[R + i], adj_recv.at[R + i], p.along("y", i))
-        afull[p.at["y"]] = arecv[...]
+        for i in range(1, X):
+            remote(arecv, afull.at[p.at["x"]], adj_send.at[R + i], adj_recv.at[R + i], p.along("x", i))
+        afull[p.at["x"]] = arecv[...]
 
     def wait_adjacency():
-        for i in range(1, Y):
-            source = lax.rem(p.at["y"] + Y - i, Y)
+        for i in range(1, X):
+            source = lax.rem(p.at["x"] + X - i, X)
             arrived(afull.at[source], adj_send.at[R + i], adj_recv.at[R + i])
 
     def build(chip, carry):
@@ -276,47 +280,40 @@
         return carry
 
     def gathered(step):
-        for direction in range(2):
-            block = gall.at[direction, origin(direction, step) * 2 + 1 - p.c]
-            arrived(block, sib_send.at[direction, step], sib_recv.at[direction, step])
         for t in range(2):
-            chip = origin(t, step)
-            halves = []
-            for core in range(2):
-                region = chip * 2 + core
-                halves.append(jnp.where(table[2, region] == 0, gall[t, region, :TILE], gall[t, region, TILE:]))
-            more = dot(bmat[chip], jnp.concatenate(halves, axis=0), (1, 0))
-            acc[t] = more if step == 0 else acc[t] + more
-
-    for item in get_cot:
-        item.wait()
-    pl.semaphore_wait(barrier, len(partners))
-    ring(0)
+            for direction in range(2):
+                if step > (Z // 2 if t == direction else Z // 2 - 1) or (step == 0 and direction == 1):
+                    continue
+                chip = origin(direction, step)
+                arrived(gall.at[t, chip * 2 + 1 - p.c], sib_send.at[direction, t, step], sib_recv.at[direction, t, step])
+                halves = []
+                for core in range(2):
+                    region = chip * 2 + core
+                    halves.append(jnp.where(table[2, region] == 0, gall[t, region, :TILE], gall[t, region, TILE:]))
+                more = dot(bmat[chip], jnp.concatenate(halves, axis=0), (1, 0))
+                acc[t] = more if step == 0 else acc[t] + more
+
     lax.fori_loop(0, R, scan, 0)
     get_adj.wait()
     lax.fori_loop(0, R, fill, 0)
-    send_adjacency()
-    ring(1)
-    for item in (get_x, get_wf, get_wg):
+    for item in (get_x, get_wf, get_wg, *get_cot):
         item.wait()
     forward(0)
-    ring(2)
-    share_adjacency()
+    pl.semaphore_wait(barrier, len(partners))
+    send_adjacency()
+    ring(0)
     forward(1)
+    ring(1)
     get_wm.wait()
-    ring(3)
     own_products()
-    work = [wait_adjacency, lambda: lax.fori_loop(0, Z, build, 0)]
-    work += [functools.partial(gathered, step) for step in range(Z - 1)]
-    per_step = -(-len(work) // max(1, Z - 4))
-    for step in range(4, Z):
+    for step in range(2, Z // 2 + 1):
         ring(step)
-        for item in work[:per_step]:
-            item()
-        work = work[per_step:]
-    for item in work:
-        item()
-    gathered(Z - 1)
+        if step == 2:
+            share_adjacency()
+    wait_adjacency()
+    lax.fori_loop(0, Z, build, 0)
+    for step in range(Z // 2 + 1):
+        gathered(step)
 
     groups = [
         Reduction(p, order, part, 2 * i, factor, scratch[i], sems[i], sends) for i, order in enumerate(ORDERS)
@@ -332,31 +329,42 @@
         part[2 + 2 * g] = dot(x_ref[0], actcot[g, 0], (0, 0)) + dot(x_ref[1], actcot[g, 1], (0, 0))
         part[3 + 2 * g] = dot(x_ref[0], actcot[g, 1], (0, 0))
         groups[1 + g].start_core()
+    late, also, early = groups
     for group in groups:
         group.start_first()
     for t in range(2):
         total = gall[t, p.region].astype(F32)
         for tap in range(2 - t):
             total = total + dot(actcot[0, t + tap], wf[tap], (1, 1)) + dot(actcot[1, t + tap], wg[tap], (1, 1))
-        gi_ref[t] = total.astype(BF16)
-    for stage in ("start_second", "start_third", "start_gather_second", "start_gather_first", "start_gather_core"):
-        for group in groups:
+        gi_vmem[t] = total.astype(BF16)
+    puts = [pltpu.make_async_copy(gi_vmem, gi_ref, local_sem.at[7])]
+    puts[0].start()
+    for stage in ("start_second", "start_third", "start_gather_second"):
+        for group in (early, late, also):
             getattr(group, stage)()
-    for group in groups:
-        group.finish(out_ref)
+    for group in (late, also, early):
+        group.start_gather_first()
+    for group in (early, late, also):
+        group.start_gather_core()
+    outs = [out_mix, out_filter, out_gate]
+    for group in (early, late, also):
+        puts += group.put(outs[groups.index(group)], put_sem, 0)
+    for group in (early, late, also):
+        group.wait()
+        puts += group.put(outs[groups.index(group)], put_sem, 1)
+    for item in puts:
+        item.wait()
     for item in sends:
         item.wait_send()
 
 
-def write(gi, grads, gi_out, gf_out, gg_out, gm_out, sem):
-    copies = [
-        pltpu.make_async_copy(gi, gi_out, sem.at[0]),
-        pltpu.make_async_copy(grads.at[pl.ds(0, 2)], gm_out, sem.at[1]),
-        pltpu.make_async_copy(grads.at[pl.ds(2, 2)], gf_out, sem.at[2]),
-        pltpu.make_async_copy(grads.at[pl.ds(4, 2)], gg_out, sem.at[3]),
-    ]
-    for item in copies:
-        item.start()
+def write(gi, mix, filt, gate, gi_out, mix_out, filt_out, gate_out, wide, sem):
+    copies = [pltpu.make_async_copy(gi, gi_out, sem.at[3])]
+    copies[0].start()
+    for i, (source, out) in enumerate(((mix, mix_out), (filt, filt_out), (gate, gate_out))):
+        wide[i] = source[...].astype(F32)
+        copies.append(pltpu.make_async_copy(wide.at[i], out, sem.at[i]))
+        copies[-1].start()
     for item in copies:
         item.wait()
 
@@ -398,30 +406,31 @@
         weights = pltpu.VMEM((2, chans, chans), BF16)
         wide = pltpu.VMEM((steps, sites, chans), F32)
         narrow = pltpu.VMEM((steps, sites, chans), BF16)
-        grad_inputs, grads = pl.pallas_call(
+        shapes = [(2, 2, sizes[order[0]], TILE // sizes[order[0]], chans) for order in ORDERS]
+        grad_inputs, *grads = pl.pallas_call(
             functools.partial(kernel, Y, Z, 1.0 / math.sqrt(total_rows)),
-            out_shape=(
-                jax.ShapeDtypeStruct((steps, sites, chans), BF16), jax.ShapeDtypeStruct((6, chans, chans), F32),
-            ),
+            out_shape=[
+                jax.ShapeDtypeStruct(shape, BF16) for shape in [(steps, sites, chans), *shapes]
+            ],
             in_specs=[pl.BlockSpec(memory_space=pltpu.SMEM)] + [hbm] * 6,
-            out_specs=(vmem, vmem),
+            out_specs=[hbm] * 4,
             scratch_shapes=[
-                narrow, weights, weights, weights,
+                narrow, dma((2, 6)), narrow, weights, weights, weights,
                 pltpu.VMEM((2 * per_tile, TILE, TILE), BF16),
                 pltpu.VMEM((steps, R, sites, chans), BF16),
-                pltpu.VMEM((R, TILE // Y, TILE), BF16),
-                pltpu.VMEM((R, TILE // Y, TILE), BF16),
-                pltpu.VMEM((Y, R, TILE // Y, TILE), BF16),
+                pltpu.VMEM((R, TILE // X, TILE), BF16),
+                pltpu.VMEM((R, TILE // X, TILE), BF16),
+                pltpu.VMEM((X, R, TILE // X, TILE), BF16),
                 pltpu.VMEM((Z, 2 * TILE, 2 * TILE), BF16),
                 wide, wide, narrow, wide, wide,
                 pltpu.VMEM((2, steps, sites, chans), BF16),
                 pltpu.VMEM((6, chans, chans), F32),
                 pltpu.SMEM((4, R), jnp.int32),
                 *scratch,
-                dma((7,)),
-                dma((2, Z, CHUNKS)), dma((2, Z, CHUNKS)),
-                dma((2, Z)), dma((2, Z)),
-                dma((R + Y,)), dma((R + Y,)),
+                dma((8,)),
+                dma((2, 2, Z // 2, 2)), dma((2, 2, Z // 2, 2)),
+                dma((2, 2, Z // 2 + 1)), dma((2, 2, Z // 2 + 1)),
+                dma((R + X,)), dma((R + X,)),
                 *sems,
             ],
             compiler_params=pltpu.CompilerParams(
@@ -430,14 +439,14 @@
         )(neighbours.T, inputs[0], cotangent[0], w_filter, w_gate, w_mix,
           adjacency.reshape(2 * per_tile, TILE, TILE))
         grad = jax.ShapeDtypeStruct((2, chans, chans), F32)
-        grad_inputs, grad_filter, grad_gate, grad_mix = pl.pallas_call(
+        grad_inputs, grad_mix, grad_filter, grad_gate = pl.pallas_call(
             write,
             out_shape=(jax.ShapeDtypeStruct((steps, sites, chans), BF16), grad, grad, grad),
-            in_specs=[pl.BlockSpec(memory_space=pl.ANY)] * 2,
+            in_specs=[vmem] * 4,
             out_specs=(hbm,) * 4,
-            scratch_shapes=[dma((4,))],
+            scratch_shapes=[pltpu.VMEM((3, 2, chans, chans), F32), dma((4,))],
             name="write",
-        )(grad_inputs, grads)
+        )(grad_inputs, *[block.reshape(2, chans, chans) for block in grads])
         return grad_inputs[None], grad_filter, grad_gate, grad_mix
 
     return jax.shard_map(

time: 143 us -> 79.7 us (0.56)
  Pallas kernels: 143 us -> 78.9 us
    pallas_call x1, Pallas kernels: 56.7 us -> 2.45 us  [per_device(): pl.pallas_call(write, out_shape=(jax.ShapeDtypeStruct((steps, sites, chan...]
    pallas_call x1, Pallas kernels: 85.9 us -> 76.4 us  [per_device(): pl.pallas_call(functools.partial(kernel, Y, Z, 1.0 / math.sqrt(total_rows...]
where the time goes in v3:
time: 79.7 us; the launch traced here: 79.5 us
  Pallas kernels  78.9 us (99%)
    pallas_call x1, Pallas kernels, per_device(): pl.pallas_call(functools.partial(kernel, Y, Z, 1.0 / math.sqrt(total_rows...  76.4 us
    pallas_call x1, Pallas kernels, per_device(): pl.pallas_call(write, out_shape=(jax.ShapeDtypeStruct((steps, sites, chan...  2.45 us

profile of v3, /device:TPU:1, one launch (start us, length us, event | category | flops | bytes accessed | tf_op | source)
XLA Modules:
  0.0 79.5 jit_solution(5602268037249619883)
XLA Ops:
  0.6 76.4 %train_step.1 = (bf16[2,256,256]{2,1,0:T(8,128)(2,1)}, bf16[2,2,8,16,256]{4,3,2,1,0:T(8,128)(2,1)}, bf16[2,2,8,16,256]{4,3,2,1,0:T(8,128)(2,1)}, bf16[2,2,4,32,256]{4,3,2,1,0:T(8,128)(2,1)}) custom-call(s32[6,32]{1,0:T(8,128)} %bitcast.14, bf16[2,256,256]{2,1,0:T(8,128)(2,1)} %bitcast.9, bf16[2,256,256]{2,1,0:T(8,128)(2,1)} %bitcast.10, ...), custom_call_target="tpu_custom_call" | custom-call | tf_op jit(solution)/shard_map/train_step/pallas_call | solution.py:410
  77.1 2.4 %write.1 = (bf16[2,256,256]{2,1,0:T(8,128)(2,1)}, f32[2,256,256]{2,1,0:T(8,128)}, f32[2,256,256]{2,1,0:T(8,128)}, f32[2,256,256]{2,1,0:T(8,128)}) custom-call(bf16[2,256,256]{2,1,0:T(8,128)(2,1)} %get-tuple-element.12.gi, bf16[2,256,256]{2,1,0:T(8,128)(2,1)} %bitcast.11, bf16[2,256,256]{2,1,0:T(8,128)(2,1)} %bitcast.12, bf16[2,256,256]{2,1,0:T(8,128)(2,1)} %bitcast.13), custom_call_target="tpu_custom_call" | custom-call | tf_op jit(solution)/shard_map/write/pallas_call | solution.py:442

commit v4 on v3

--- a/solution.py
+++ b/solution.py
@@ -1,4 +1,5 @@
 import functools
+import itertools
 import math
 
 import jax
@@ -147,7 +148,7 @@
 
 def kernel(Y, Z, factor, nbr, x_hbm, cot_hbm, wf_hbm, wg_hbm, wm_hbm, adj_hbm,
            gi_ref, out_mix, out_filter, out_gate,
-           gi_vmem, put_sem, x_ref, wf, wg, wm, adj, gall, asend, arecv, afull, bmat, direct, acc, hid, f1, f2, actcot, part, table,
+           gi_vmem, put_sem, x_ref, wf, wg, wm, adj, gall, asend, arecv, apair, afull, bmat, direct, acc, hid, f1, f2, actcot, part, table,
            *rest):
     scratch = [rest[9 * i:9 * i + 9] for i in range(3)]
     local_sem, ring_send, ring_recv, sib_send, sib_recv, adj_send, adj_recv = rest[27:34]
@@ -156,7 +157,8 @@
     R = 2 * Z
     per_tile = nbr.shape[0]
     entries = 2 * per_tile
-    rows = TILE // X
+    rows = TILE // (2 * X)
+    parity = lax.rem(p.at["y"], 2)
     sends = []
 
     def fetch(i, src, dst):
@@ -191,24 +193,20 @@
     def origin(direction, step):
         return lax.rem(p.at["z"] + (Z - step if direction == 0 else step), Z)
 
-    def ring(step):
-        for t in range(2):
-            for direction in range(2):
-                reach = Z // 2 if t == direction else Z // 2 - 1
-                if step > reach:
-                    continue
-                slot = origin(direction, step) * 2 + p.c
-                for tile in range(2):
-                    block = gall.at[t, slot, pl.ds(tile * TILE, TILE)]
-                    if step > 0:
-                        arrived(block, ring_send.at[direction, t, step - 1, tile],
-                                ring_recv.at[direction, t, step - 1, tile])
-                    if step < reach:
-                        remote(block, block, ring_send.at[direction, t, step, tile],
-                               ring_recv.at[direction, t, step, tile], p.along("z", 1 if direction == 0 else Z - 1))
-                if step > 0 or direction == 0:
-                    block = gall.at[t, slot]
-                    remote(block, block, sib_send.at[direction, t, step], sib_recv.at[direction, t, step], p.sibling)
+    def ring(step, times=(0, 1)):
+        for t, tile, direction in itertools.product(times, range(2), range(2)):
+            reach = Z // 2 if t == direction else Z // 2 - 1
+            if step > reach:
+                continue
+            block = gall.at[t, origin(direction, step) * 2 + p.c, pl.ds(tile * TILE, TILE)]
+            if step > 0:
+                arrived(block, ring_send.at[direction, t, step - 1, tile], ring_recv.at[direction, t, step - 1, tile])
+            if step < reach:
+                remote(block, block, ring_send.at[direction, t, step, tile], ring_recv.at[direction, t, step, tile],
+                       p.along("z", 1 if direction == 0 else Z - 1))
+            if step > 0 or direction == 0:
+                remote(block, block, sib_send.at[direction, t, step, tile], sib_recv.at[direction, t, step, tile],
+                       p.sibling)
 
     def scan(region, carry):
         entry = valid = other = mine = jnp.int32(0)
@@ -226,7 +224,7 @@
         return carry
 
     def fill(region, carry):
-        block = adj[table[0, region], pl.ds(pl.multiple_of(p.at["x"] * rows, rows), rows)]
+        block = adj[table[0, region], pl.ds(pl.multiple_of((p.at["x"] * 2 + parity) * rows, rows), rows)]
         asend[region] = jnp.where(table[1, region] == 1, block, jnp.zeros_like(block))
         return carry
 
@@ -256,13 +254,18 @@
             target = lax.rem(p.region + i, R)
             remote(asend.at[target], arecv.at[p.region], adj_send.at[i], adj_recv.at[i], (p.dp, target))
 
-    def share_adjacency():
+    def pair_adjacency():
         for i in range(1, R):
             source = lax.rem(p.region + R - i, R)
             arrived(arecv.at[source], adj_send.at[i], adj_recv.at[i])
+        remote(arecv, apair.at[parity], adj_send.at[R + X], adj_recv.at[R + X], p.along("y", 1 + (Y - 2) * parity))
+        apair[parity] = arecv[...]
+
+    def share_adjacency():
+        arrived(apair.at[1 - parity], adj_send.at[R + X], adj_recv.at[R + X])
         for i in range(1, X):
-            remote(arecv, afull.at[p.at["x"]], adj_send.at[R + i], adj_recv.at[R + i], p.along("x", i))
-        afull[p.at["x"]] = arecv[...]
+            remote(apair, afull.at[p.at["x"]], adj_send.at[R + i], adj_recv.at[R + i], p.along("x", i))
+        afull[p.at["x"]] = apair[...]
 
     def wait_adjacency():
         for i in range(1, X):
@@ -272,7 +275,7 @@
     def build(chip, carry):
         for core in range(2):
             region = chip * 2 + core
-            block = afull[:, region].reshape(TILE, TILE).T
+            block = afull[:, :, region].reshape(TILE, TILE).T
             zero = jnp.zeros_like(block)
             for j in range(2):
                 bmat[chip, j * TILE:(j + 1) * TILE, core * TILE:(core + 1) * TILE] = jnp.where(
@@ -285,7 +288,9 @@
                 if step > (Z // 2 if t == direction else Z // 2 - 1) or (step == 0 and direction == 1):
                     continue
                 chip = origin(direction, step)
-                arrived(gall.at[t, chip * 2 + 1 - p.c], sib_send.at[direction, t, step], sib_recv.at[direction, t, step])
+                for tile in range(2):
+                    arrived(gall.at[t, chip * 2 + 1 - p.c, pl.ds(tile * TILE, TILE)],
+                            sib_send.at[direction, t, step, tile], sib_recv.at[direction, t, step, tile])
                 halves = []
                 for core in range(2):
                     region = chip * 2 + core
@@ -296,24 +301,30 @@
     lax.fori_loop(0, R, scan, 0)
     get_adj.wait()
     lax.fori_loop(0, R, fill, 0)
-    for item in (get_x, get_wf, get_wg, *get_cot):
+    for item in get_cot:
+        item.wait()
+    pl.semaphore_wait(barrier, len(partners))
+    ring(0, (0,))
+    send_adjacency()
+    ring(0, (1,))
+    for item in (get_x, get_wf, get_wg):
         item.wait()
     forward(0)
-    pl.semaphore_wait(barrier, len(partners))
-    send_adjacency()
-    ring(0)
     forward(1)
+    pair_adjacency()
     ring(1)
+    share_adjacency()
     get_wm.wait()
     own_products()
-    for step in range(2, Z // 2 + 1):
+    for step in range(2, Z // 2):
         ring(step)
-        if step == 2:
-            share_adjacency()
     wait_adjacency()
     lax.fori_loop(0, Z, build, 0)
-    for step in range(Z // 2 + 1):
+    for step in range(Z // 2 - 1):
         gathered(step)
+    ring(Z // 2)
+    gathered(Z // 2 - 1)
+    gathered(Z // 2)
 
     groups = [
         Reduction(p, order, part, 2 * i, factor, scratch[i], sems[i], sends) for i, order in enumerate(ORDERS)
@@ -418,9 +429,10 @@
                 narrow, dma((2, 6)), narrow, weights, weights, weights,
                 pltpu.VMEM((2 * per_tile, TILE, TILE), BF16),
                 pltpu.VMEM((steps, R, sites, chans), BF16),
-                pltpu.VMEM((R, TILE // X, TILE), BF16),
-                pltpu.VMEM((R, TILE // X, TILE), BF16),
-                pltpu.VMEM((X, R, TILE // X, TILE), BF16),
+                pltpu.VMEM((R, TILE // (2 * X), TILE), BF16),
+                pltpu.VMEM((R, TILE // (2 * X), TILE), BF16),
+                pltpu.VMEM((2, R, TILE // (2 * X), TILE), BF16),
+                pltpu.VMEM((X, 2, R, TILE // (2 * X), TILE), BF16),
                 pltpu.VMEM((Z, 2 * TILE, 2 * TILE), BF16),
                 wide, wide, narrow, wide, wide,
                 pltpu.VMEM((2, steps, sites, chans), BF16),
@@ -429,8 +441,8 @@
                 *scratch,
                 dma((8,)),
                 dma((2, 2, Z // 2, 2)), dma((2, 2, Z // 2, 2)),
-                dma((2, 2, Z // 2 + 1)), dma((2, 2, Z // 2 + 1)),
-                dma((R + X,)), dma((R + X,)),
+                dma((2, 2, Z // 2 + 1, 2)), dma((2, 2, Z // 2 + 1, 2)),
+                dma((R + X + 1,)), dma((R + X + 1,)),
                 *sems,
             ],
             compiler_params=pltpu.CompilerParams(

time: 79.7 us -> 78 us (0.979)
  Pallas kernels: 78.9 us -> 77.2 us
    pallas_call x1, Pallas kernels: 76.4 us -> 74.8 us  [per_device(): pl.pallas_call(functools.partial(kernel, Y, Z, 1.0 / math.sqrt(total_rows...]
where the time goes in v4:
time: 78 us; the launch traced here: 77.9 us
  Pallas kernels  77.2 us (99%)
    pallas_call x1, Pallas kernels, per_device(): pl.pallas_call(functools.partial(kernel, Y, Z, 1.0 / math.sqrt(total_rows...  74.8 us
    pallas_call x1, Pallas kernels, per_device(): pl.pallas_call(write, out_shape=(jax.ShapeDtypeStruct((steps, sites, chan...  2.45 us

profile of v4, /device:TPU:1, one launch (start us, length us, event | category | flops | bytes accessed | tf_op | source)
XLA Modules:
  0.0 77.9 jit_solution(2149294476284839466)
XLA Ops:
  0.6 74.8 %train_step.1 = (bf16[2,256,256]{2,1,0:T(8,128)(2,1)}, bf16[2,2,8,16,256]{4,3,2,1,0:T(8,128)(2,1)}, bf16[2,2,8,16,256]{4,3,2,1,0:T(8,128)(2,1)}, bf16[2,2,4,32,256]{4,3,2,1,0:T(8,128)(2,1)}) custom-call(s32[6,32]{1,0:T(8,128)} %bitcast.14, bf16[2,256,256]{2,1,0:T(8,128)(2,1)} %bitcast.9, bf16[2,256,256]{2,1,0:T(8,128)(2,1)} %bitcast.10, ...), custom_call_target="tpu_custom_call" | custom-call | tf_op jit(solution)/shard_map/train_step/pallas_call | solution.py:421
  75.4 2.4 %write.1 = (bf16[2,256,256]{2,1,0:T(8,128)(2,1)}, f32[2,256,256]{2,1,0:T(8,128)}, f32[2,256,256]{2,1,0:T(8,128)}, f32[2,256,256]{2,1,0:T(8,128)}) custom-call(bf16[2,256,256]{2,1,0:T(8,128)(2,1)} %get-tuple-element.12.gi, bf16[2,256,256]{2,1,0:T(8,128)(2,1)} %bitcast.11, bf16[2,256,256]{2,1,0:T(8,128)(2,1)} %bitcast.12, bf16[2,256,256]{2,1,0:T(8,128)(2,1)} %bitcast.13), custom_call_target="tpu_custom_call" | custom-call | tf_op jit(solution)/shard_map/write/pallas_call | solution.py:454

commit v5 on v4

--- a/solution.py
+++ b/solution.py
@@ -148,7 +148,7 @@
 
 def kernel(Y, Z, factor, nbr, x_hbm, cot_hbm, wf_hbm, wg_hbm, wm_hbm, adj_hbm,
            gi_ref, out_mix, out_filter, out_gate,
-           gi_vmem, put_sem, x_ref, wf, wg, wm, adj, gall, asend, arecv, apair, afull, bmat, direct, acc, hid, f1, f2, actcot, part, table,
+           gi_vmem, put_sem, x_ref, wf, wg, wm, adj, gall, asend, arecv, apair, afull, bmat, direct, acc, hid, hid_t, x_t, wm_t, f1, f2, actcot, part, table,
            *rest):
     scratch = [rest[9 * i:9 * i + 9] for i in range(3)]
     local_sem, ring_send, ring_recv, sib_send, sib_recv, adj_send, adj_recv = rest[27:34]
@@ -238,14 +238,17 @@
         gate = jax.nn.sigmoid(pre_g)
         both = filt * gate
         hid[t] = both.astype(BF16)
+        hid_t[t] = hid[t].T
+        x_t[t] = x_ref[t].T
         f1[t] = gate * (1.0 - filt * filt)
         f2[t] = both * (1.0 - gate)
 
     def own_products():
+        wm_t[...] = wm[1].T
         for t in range(2):
             cot = gall[t, p.region]
             direct[t] = dot(cot, wm[0], (1, 1))
-            here = dot(hid[t], cot, (0, 0))
+            here = dot(hid_t[t], cot, (1, 0))
             part[0] = here if t == 0 else part[0] + here
 
     def send_adjacency():
@@ -258,19 +261,24 @@
         for i in range(1, R):
             source = lax.rem(p.region + R - i, R)
             arrived(arecv.at[source], adj_send.at[i], adj_recv.at[i])
-        remote(arecv, apair.at[parity], adj_send.at[R + X], adj_recv.at[R + X], p.along("y", 1 + (Y - 2) * parity))
-        apair[parity] = arecv[...]
+        remote(arecv, apair, adj_send.at[R], adj_recv.at[R], p.along("y", 1 + (Y - 2) * parity))
+        spread(arecv, parity, R)
+        afull[p.at["x"], parity] = arecv[...]
+
+    def spread(block, half, base):
+        for i in range(1, X):
+            remote(block, afull.at[p.at["x"], half], adj_send.at[base + i], adj_recv.at[base + i], p.along("x", i))
 
     def share_adjacency():
-        arrived(apair.at[1 - parity], adj_send.at[R + X], adj_recv.at[R + X])
-        for i in range(1, X):
-            remote(apair, afull.at[p.at["x"]], adj_send.at[R + i], adj_recv.at[R + i], p.along("x", i))
-        afull[p.at["x"]] = apair[...]
+        arrived(apair, adj_send.at[R], adj_recv.at[R])
+        spread(apair, 1 - parity, R + X)
+        afull[p.at["x"], 1 - parity] = apair[...]
 
     def wait_adjacency():
-        for i in range(1, X):
-            source = lax.rem(p.at["x"] + X - i, X)
-            arrived(afull.at[source], adj_send.at[R + i], adj_recv.at[R + i])
+        for half, base in ((parity, R), (1 - parity, R + X)):
+            for i in range(1, X):
+                source = lax.rem(p.at["x"] + X - i, X)
+                arrived(afull.at[source, half], adj_send.at[base + i], adj_recv.at[base + i])
 
     def build(chip, carry):
         for core in range(2):
@@ -298,51 +306,65 @@
                 more = dot(bmat[chip], jnp.concatenate(halves, axis=0), (1, 0))
                 acc[t] = more if step == 0 else acc[t] + more
 
+    for item in get_cot:
+        item.wait()
+    pl.semaphore_wait(barrier, len(partners))
+    ring(0)
     lax.fori_loop(0, R, scan, 0)
     get_adj.wait()
     lax.fori_loop(0, R, fill, 0)
-    for item in get_cot:
-        item.wait()
-    pl.semaphore_wait(barrier, len(partners))
-    ring(0, (0,))
     send_adjacency()
-    ring(0, (1,))
     for item in (get_x, get_wf, get_wg):
         item.wait()
     forward(0)
+    ring(1, (0,))
     forward(1)
+    ring(1, (1,))
     pair_adjacency()
-    ring(1)
+    ring(2, (0,))
     share_adjacency()
     get_wm.wait()
     own_products()
-    for step in range(2, Z // 2):
-        ring(step)
+    ring(2, (1,))
+    for step in range(3, Z // 2):
+        ring(step, (0,))
+        ring(step, (1,))
     wait_adjacency()
     lax.fori_loop(0, Z, build, 0)
     for step in range(Z // 2 - 1):
         gathered(step)
-    ring(Z // 2)
+    if Z > 4:
+        ring(Z // 2)
     gathered(Z // 2 - 1)
     gathered(Z // 2)
 
+    def settle(items):
+        for item in items:
+            item.wait_send()
+
+    def taken():
+        items = list(sends)
+        sends.clear()
+        return items
+
+    before = taken()
     groups = [
         Reduction(p, order, part, 2 * i, factor, scratch[i], sems[i], sends) for i, order in enumerate(ORDERS)
     ]
     mixed = [acc[t].astype(BF16) for t in range(2)]
-    part[1] = dot(hid[0], mixed[0], (0, 0)) + dot(hid[1], mixed[1], (0, 0))
+    part[1] = dot(hid_t[0], mixed[0], (1, 0)) + dot(hid_t[1], mixed[1], (1, 0))
     groups[0].start_core()
     for t in range(2):
-        grad = direct[t] + dot(mixed[t], wm[1], (1, 1))
+        grad = direct[t] + dot(mixed[t], wm_t[...], (1, 0))
         actcot[0, t] = (grad * f1[t]).astype(BF16)
         actcot[1, t] = (grad * f2[t]).astype(BF16)
     for g in range(2):
-        part[2 + 2 * g] = dot(x_ref[0], actcot[g, 0], (0, 0)) + dot(x_ref[1], actcot[g, 1], (0, 0))
-        part[3 + 2 * g] = dot(x_ref[0], actcot[g, 1], (0, 0))
+        part[2 + 2 * g] = dot(x_t[0], actcot[g, 0], (1, 0)) + dot(x_t[1], actcot[g, 1], (1, 0))
+        part[3 + 2 * g] = dot(x_t[0], actcot[g, 1], (1, 0))
         groups[1 + g].start_core()
+        groups[g].start_first()
+    groups[2].start_first()
     late, also, early = groups
-    for group in groups:
-        group.start_first()
     for t in range(2):
         total = gall[t, p.region].astype(F32)
         for tap in range(2 - t):
@@ -350,33 +372,39 @@
         gi_vmem[t] = total.astype(BF16)
     puts = [pltpu.make_async_copy(gi_vmem, gi_ref, local_sem.at[7])]
     puts[0].start()
-    for stage in ("start_second", "start_third", "start_gather_second"):
-        for group in (early, late, also):
-            getattr(group, stage)()
-    for group in (late, also, early):
-        group.start_gather_first()
-    for group in (early, late, also):
-        group.start_gather_core()
+    settle(before)
+    stages = [
+        (name, (early, late, also)) for name in ("start_second", "start_third", "start_gather_second")
+    ] + [("start_gather_first", (late, also, early)), ("start_gather_core", (early, late, also))]
+    for name, order in stages:
+        before = taken()
+        for group in order:
+            getattr(group, name)()
+        settle(before)
     outs = [out_mix, out_filter, out_gate]
     for group in (early, late, also):
         puts += group.put(outs[groups.index(group)], put_sem, 0)
     for group in (early, late, also):
         group.wait()
         puts += group.put(outs[groups.index(group)], put_sem, 1)
+    settle(sends)
     for item in puts:
         item.wait()
-    for item in sends:
-        item.wait_send()
-
-
-def write(gi, mix, filt, gate, gi_out, mix_out, filt_out, gate_out, wide, sem):
-    copies = [pltpu.make_async_copy(gi, gi_out, sem.at[3])]
-    copies[0].start()
-    for i, (source, out) in enumerate(((mix, mix_out), (filt, filt_out), (gate, gate_out))):
-        wide[i] = source[...].astype(F32)
-        copies.append(pltpu.make_async_copy(wide.at[i], out, sem.at[i]))
-        copies[-1].start()
-    for item in copies:
+
+
+def write(gi, mix, filt, gate, gi_out, mix_out, filt_out, gate_out, gi_vmem, narrow, wide, sem):
+    gets = [pltpu.make_async_copy(ref, narrow.at[i], sem.at[i]) for i, ref in enumerate((mix, filt, gate))]
+    gets.append(pltpu.make_async_copy(gi, gi_vmem, sem.at[3]))
+    for item in gets:
+        item.start()
+    puts = [pltpu.make_async_copy(wide.at[i], ref, sem.at[4 + i]) for i, ref in enumerate((mix_out, filt_out, gate_out))]
+    puts.append(pltpu.make_async_copy(gi_vmem, gi_out, sem.at[7]))
+    for i in range(4):
+        gets[i].wait()
+        if i < 3:
+            wide[i] = narrow[i].astype(F32)
+        puts[i].start()
+    for item in puts:
         item.wait()
 
 
@@ -429,12 +457,10 @@
                 narrow, dma((2, 6)), narrow, weights, weights, weights,
                 pltpu.VMEM((2 * per_tile, TILE, TILE), BF16),
                 pltpu.VMEM((steps, R, sites, chans), BF16),
-                pltpu.VMEM((R, TILE // (2 * X), TILE), BF16),
-                pltpu.VMEM((R, TILE // (2 * X), TILE), BF16),
-                pltpu.VMEM((2, R, TILE // (2 * X), TILE), BF16),
+                *[pltpu.VMEM((R, TILE // (2 * X), TILE), BF16)] * 3,
                 pltpu.VMEM((X, 2, R, TILE // (2 * X), TILE), BF16),
                 pltpu.VMEM((Z, 2 * TILE, 2 * TILE), BF16),
-                wide, wide, narrow, wide, wide,
+                wide, wide, narrow, narrow, narrow, pltpu.VMEM((chans, chans), BF16), wide, wide,
                 pltpu.VMEM((2, steps, sites, chans), BF16),
                 pltpu.VMEM((6, chans, chans), F32),
                 pltpu.SMEM((4, R), jnp.int32),
@@ -442,7 +468,7 @@
                 dma((8,)),
                 dma((2, 2, Z // 2, 2)), dma((2, 2, Z // 2, 2)),
                 dma((2, 2, Z // 2 + 1, 2)), dma((2, 2, Z // 2 + 1, 2)),
-                dma((R + X + 1,)), dma((R + X + 1,)),
+                dma((R + 2 * X,)), dma((R + 2 * X,)),
                 *sems,
             ],
             compiler_params=pltpu.CompilerParams(
@@ -454,9 +480,11 @@
         grad_inputs, grad_mix, grad_filter, grad_gate = pl.pallas_call(
             write,
             out_shape=(jax.ShapeDtypeStruct((steps, sites, chans), BF16), grad, grad, grad),
-            in_specs=[vmem] * 4,
+            in_specs=[hbm] * 4,
             out_specs=(hbm,) * 4,
-            scratch_shapes=[pltpu.VMEM((3, 2, chans, chans), F32), dma((4,))],
+            scratch_shapes=[
+                narrow, pltpu.VMEM((3, 2, chans, chans), BF16), pltpu.VMEM((3, 2, chans, chans), F32), dma((8,)),
+            ],
             name="write",
         )(grad_inputs, *[block.reshape(2, chans, chans) for block in grads])
         return grad_inputs[None], grad_filter, grad_gate, grad_mix

time: 78 us -> 77.4 us (level)
  no operation moved by 1% of the time
where the time goes in v5:
time: 77.4 us; the launch traced here: 77.2 us
  Pallas kernels  76.6 us (99%)
    pallas_call x1, Pallas kernels, per_device(): pl.pallas_call(functools.partial(kernel, Y, Z, 1.0 / math.sqrt(total_rows...  74.3 us
    pallas_call x1, Pallas kernels, per_device(): pl.pallas_call(write, out_shape=(jax.ShapeDtypeStruct((steps, sites, chan...  2.28 us

profile of v5, /device:TPU:1, one launch (start us, length us, event | category | flops | bytes accessed | tf_op | source)
XLA Modules:
  0.0 77.2 jit_solution(746012031016589988)
XLA Ops:
  0.6 74.3 %train_step.1 = (bf16[2,256,256]{2,1,0:T(8,128)(2,1)}, bf16[2,2,8,16,256]{4,3,2,1,0:T(8,128)(2,1)}, bf16[2,2,8,16,256]{4,3,2,1,0:T(8,128)(2,1)}, bf16[2,2,4,32,256]{4,3,2,1,0:T(8,128)(2,1)}) custom-call(s32[6,32]{1,0:T(8,128)} %bitcast.14, bf16[2,256,256]{2,1,0:T(8,128)(2,1)} %bitcast.9, bf16[2,256,256]{2,1,0:T(8,128)(2,1)} %bitcast.10, ...), custom_call_target="tpu_custom_call" | custom-call | tf_op jit(solution)/shard_map/train_step/pallas_call | solution.py:449
  75.0 2.3 %write.1 = (bf16[2,256,256]{2,1,0:T(8,128)(2,1)}, f32[2,256,256]{2,1,0:T(8,128)}, f32[2,256,256]{2,1,0:T(8,128)}, f32[2,256,256]{2,1,0:T(8,128)}) custom-call(bf16[2,256,256]{2,1,0:T(8,128)(2,1)} %get-tuple-element.12.gi, bf16[2,256,256]{2,1,0:T(8,128)(2,1)} %bitcast.11, bf16[2,256,256]{2,1,0:T(8,128)(2,1)} %bitcast.12, bf16[2,256,256]{2,1,0:T(8,128)(2,1)} %bitcast.13), custom_call_target="tpu_custom_call" | custom-call | tf_op jit(solution)/shard_map/write/pallas_call | solution.py:480

commit v6 on v5

--- a/solution.py
+++ b/solution.py
@@ -131,10 +131,15 @@
             self.g1[at, i] = jnp.concatenate(rows, axis=0).astype(BF16)
         for i, slot, device in peers:
             self.copy(self.g1.at[at], self.g1.at[at], device)
+        self.gathered, self.items = self.items, []
+        self.copy(self.g1.at[at], self.cg.at[at], self.p.sibling)
 
     def start_gather_core(self):
-        self.wait()
-        self.copy(self.g1, self.cg, self.p.sibling)
+        n, at, _ = self.peers(0)
+        for i, item in enumerate(self.gathered, 1):
+            item.wait_recv()
+            slot = lax.rem(at + n - i, n)
+            self.copy(self.g1.at[slot], self.cg.at[slot], self.p.sibling)
 
     def put(self, out, sem, other):
         source, core = (self.cg, 1 - self.p.c) if other else (self.g1, self.p.c)
@@ -440,7 +445,7 @@
         for order in ORDERS:
             scratch += reduction_scratch(order, chans, sizes)
             n1, n2, n3 = (sizes[axis] for axis in order)
-            count = 2 + 2 * (n1 - 1) + 2 * (n2 - 1) + n3 - 1
+            count = 2 + 3 * (n1 - 1) + 2 * (n2 - 1) + n3 - 1
             sems += [dma((count,)), dma((count,))]
         weights = pltpu.VMEM((2, chans, chans), BF16)
         wide = pltpu.VMEM((steps, sites, chans), F32)

time: 77.4 us -> 77.7 us (level)
  no operation moved by 1% of the time
where the time goes in v6:
time: 77.7 us; the launch traced here: 77.5 us
  Pallas kernels  76.9 us (99%)
    pallas_call x1, Pallas kernels, per_device(): pl.pallas_call(functools.partial(kernel, Y, Z, 1.0 / math.sqrt(total_rows...  74.6 us
    pallas_call x1, Pallas kernels, per_device(): pl.pallas_call(write, out_shape=(jax.ShapeDtypeStruct((steps, sites, chan...  2.28 us

profile of v6, /device:TPU:1, one launch (start us, length us, event | category | flops | bytes accessed | tf_op | source)
XLA Modules:
  0.0 77.5 jit_solution(11401076577540796524)
XLA Ops:
  0.6 74.6 %train_step.1 = (bf16[2,256,256]{2,1,0:T(8,128)(2,1)}, bf16[2,2,8,16,256]{4,3,2,1,0:T(8,128)(2,1)}, bf16[2,2,8,16,256]{4,3,2,1,0:T(8,128)(2,1)}, bf16[2,2,4,32,256]{4,3,2,1,0:T(8,128)(2,1)}) custom-call(s32[6,32]{1,0:T(8,128)} %bitcast.14, bf16[2,256,256]{2,1,0:T(8,128)(2,1)} %bitcast.9, bf16[2,256,256]{2,1,0:T(8,128)(2,1)} %bitcast.10, ...), custom_call_target="tpu_custom_call" | custom-call | tf_op jit(solution)/shard_map/train_step/pallas_call | solution.py:454
  75.2 2.3 %write.1 = (bf16[2,256,256]{2,1,0:T(8,128)(2,1)}, f32[2,256,256]{2,1,0:T(8,128)}, f32[2,256,256]{2,1,0:T(8,128)}, f32[2,256,256]{2,1,0:T(8,128)}) custom-call(bf16[2,256,256]{2,1,0:T(8,128)(2,1)} %get-tuple-element.12.gi, bf16[2,256,256]{2,1,0:T(8,128)(2,1)} %bitcast.11, bf16[2,256,256]{2,1,0:T(8,128)(2,1)} %bitcast.12, bf16[2,256,256]{2,1,0:T(8,128)(2,1)} %bitcast.13), custom_call_target="tpu_custom_call" | custom-call | tf_op jit(solution)/shard_map/write/pallas_call | solution.py:485
